TPU v7x, 256 devices: a whole 4x4x8 slice. The times are simulated.
256 devices in a mesh: row: 16 (over z, y_lo), col: 16 (over y_hi, x, core).
Axes of the slice: x: 4, y: 4 (y_hi: 2, y_lo: 2; y = y_hi * 2 + y_lo), z: 8, core: 2. Of those that a mesh axis runs over, the one named last changes fastest.
Arguments:
- core_blocks: float32 [64, 2048, 128], P('row', 'col'), may hold values from -6 to 6
- block_coords: int32 [64, 32], replicated, may hold values from 0 to 9, as said below
- band_vectors: float32 [16, 16, 128], P('col'), may hold values from -6 to 6
- band_blocks: int32 [16, 16], P('col'), may hold values from 0 to 159, as said below
- spread: float32 [], replicated, may hold values from 12 to 24
Outputs:
- purified: float32 [64, 2048, 128], P('row', 'col')
Inputs may be any that keep to these rules, and one draw needn't show every extreme that they name: `block_coords`: the first entry of a slot is a local block row below 10, the second a local block column below 10; the 4 slots of one tile name distinct blocks. `band_blocks`: the 16 block rows of one band are distinct.
All inputs are finite; a program needn't handle non-finite values.
Results may differ from a plain program's by a relative error of at most 0.0003.
Values sent between devices are 32-bit elements; how exact they have to be, the bound alone decides.
A program may use at most 64 MiB of HBM per device.

v0:
```python
import jax
import jax.numpy as jnp
from jax import lax
from jax.sharding import PartitionSpec as P

NB = 160


highest = lax.Precision.HIGHEST


def shifted(block, axis, distance):
    devices = range(lax.axis_size(axis))
    route = [((i - distance) % len(devices), i) for i in devices]
    return lax.ppermute(block, axis, route)


def exchange_term(vectors, blocks, block_rows, block_cols):
    hit_row = (blocks[:, :, None] == block_rows[None, None, :]).astype(jnp.float32)
    hit_col = (blocks[:, :, None] == block_cols[None, None, :]).astype(jnp.float32)
    vec_row = jnp.einsum("bln,blx->bnx", hit_row, vectors, precision=highest)
    vec_col = jnp.einsum("bln,blx->bnx", hit_col, vectors, precision=highest)
    return -jnp.einsum("bnx,bny->nxy", vec_row, vec_col, precision=highest)


def tile_layout(layout, tile_row, tile_col):
    slots = layout.shape[1]
    start = (tile_row, jnp.int32(0), tile_col, jnp.int32(0))
    return lax.dynamic_slice(layout, start, (1, slots, 1, 2)).reshape(slots, 2)


def link_weights(targets, left_local, piece, right_local, tile_rows):
    row_target = targets[:, None, None, 0]
    col_target = targets[:, None, None, 1]
    row_left = left_local[None, :, None, 0]
    col_left = left_local[None, :, None, 1]
    row_right = right_local[None, None, :, 0]
    col_right = right_local[None, None, :, 1]
    keep = (row_left == row_target) & (col_left // tile_rows == piece)
    keep = keep & (col_left % tile_rows == row_right) & (col_right == col_target)
    return keep.astype(jnp.float32)


def accumulate(
    total, targets, left_blocks, left_local, piece, right_blocks, right_local, tile_rows
):
    weight = link_weights(targets, left_local, piece, right_local, tile_rows)
    pairs = jnp.einsum("axk,bky->axby", left_blocks, right_blocks, precision=highest)
    return total + jnp.einsum("tab,axby->txy", weight, pairs, precision=highest)


def advance(window):
    moved = shifted(window[0], "col", -1)
    return jnp.concatenate([window[1:], moved[None]], axis=0)


def align_right(right, this_col, ratio):
    row_count = lax.axis_size("row")
    amount = ratio * this_col % row_count
    for place in range((row_count - 1).bit_length()):
        moved = shifted(right, "row", -(1 << place))
        right = jnp.where(amount >> place & 1 == 1, moved, right)
    return right


def align_left(left, this_row, ratio):
    column_count = lax.axis_size("col")
    window = jnp.stack([left] * ratio)
    amount = this_row // ratio
    for place in range((column_count - 1).bit_length()):
        moved = shifted(window, "col", -(1 << place))
        window = jnp.where(amount >> place & 1 == 1, moved, window)
    return window


def shifted_product(left, right, layout, targets, this_row, this_col, tile_rows, ratio):
    row_count = lax.axis_size("row")
    window = align_left(left, this_row, ratio)

    def step_body(step, carry):
        total, window, right = carry
        source = (this_row + ratio * this_col + step) % row_count
        left_local = tile_layout(layout, this_row, source // ratio)
        right_local = tile_layout(layout, source, this_col)
        total = accumulate(
            total, targets, window[0], left_local, source % ratio, right, right_local, tile_rows
        )
        window = advance(window)
        right = shifted(right, "row", -1)
        return (total, window, right)

    total, window, right = lax.fori_loop(
        0, row_count, step_body, (jnp.zeros_like(left), window, right)
    )
    return (total, right)


def on_device(core_blocks, block_coords, band_vectors, band_blocks, spread):
    row_count = lax.axis_size("row")
    column_count = lax.axis_size("col")
    tile_rows = NB // row_count
    tile_columns = NB // column_count
    ratio = row_count // column_count
    slots = core_blocks.shape[0]
    this_row = lax.axis_index("row")
    this_col = lax.axis_index("col")
    layout = block_coords.reshape(row_count, slots, column_count, 2)
    targets = tile_layout(layout, this_row, this_col)
    vectors, blocks = (
        lax.all_gather(band_vectors, "col", axis=0, tiled=True),
        lax.all_gather(band_blocks, "col", axis=0, tiled=True),
    )
    block_rows = this_row * tile_rows + targets[:, 0]
    block_cols = this_col * tile_columns + targets[:, 1]
    exchange = exchange_term(vectors, blocks, block_rows, block_cols)
    fock = core_blocks + exchange
    scaled = fock / spread
    right = align_right(scaled, this_col, ratio)
    square, right = shifted_product(
        scaled, right, layout, targets, this_row, this_col, tile_rows, ratio
    )
    cube, right = shifted_product(
        square, right, layout, targets, this_row, this_col, tile_rows, ratio
    )
    return 1.5 * fock - 2.0 * spread * cube


def solution(mesh):
    placed = (P("row", "col", None), P(), P("col", None, None), P("col", None), P())
    return jax.shard_map(
        on_device, mesh=mesh, in_specs=placed, out_specs=P("row", "col", None), check_vma=False
    )
```

profile of v0, /device:TPU:1, one launch (start us, length us, event | category | flops | bytes accessed | tf_op | source)
XLA Modules:
  0.0 535.8 jit_solution(16270872847556958908)
XLA Ops:
  1.4 26.0 %all_gather.7 = f32[16,16,128]{2,1,0:T(8,128)S(1)} all-gather(f32[1,16,128]{2,1,0:T(8,128)S(1)} %copy-done.1), channel_id=1, replica_groups=mesh['row'=16,'col'=16] {'col'}, dimensions={0}, use_global_device_ids=true | all-gather | bytes 139264 | tf_op jit(solution)/shard_map/all_gather | solution.py:110
  28.0 19.3 %all-gather = s32[16,1,16]{2,1,0:T(1,128)S(1)} all-gather(s32[1,1,16]{2,1,0:T(1,128)S(1)} %bitcast.174), channel_id=1, replica_groups=mesh['row'=16,'col'=16] {'col'}, dimensions={0}, use_global_device_ids=true | all-gather | bytes 1088 | tf_op jit(solution)/shard_map/all_gather | solution.py:111
  49.1 5.8 %collective-permute-start.8 = (f32[4,128,128]{2,1,0:T(8,128)S(1)}, f32[4,128,128]{2,1,0:T(8,128)S(1)}, u32[]{:S(2)}, u32[]{:S(2)}) collective-permute-start(f32[4,128,128]{2,1,0:T(8,128)S(1)} %get-tuple-element.699), channel_id=1, source_target_pairs={{16,0},{32,16},{48,32},{64,48},{80,64},{96,80},{112,96},{128,112},... | collective-permute-start | bytes 786440 | tf_op jit(solution)/shard_map/ppermute | solution.py:15
  55.3 5.0 collective-permute-done.8
  62.6 4.3 collective-permute-start.5
  73.6 4.7 collective-permute-done.10
  78.3 4.8 collective-permute-start.11
  84.5 10.0 %collective-permute-done.11 = f32[4,128,128]{2,1,0:T(8,128)S(1)} collective-permute-done((f32[4,128,128]{2,1,0:T(8,128)S(1)}, f32[4,128,128]{2,1,0:T(8,128)S(1)}, u32[]{:S(2)}, u32[]{:S(2)}) %collective-permute-start.11) | collective-permute-done | bytes 262176 | tf_op jit(solution)/shard_map/ppermute | solution.py:15
  94.6 201.8 %while.42 = (s32[]{:T(128)}, f32[4,128,128]{2,0,1:T(4,128)S(1)}, f32[1,4,128,128]{3,2,1,0:T(8,128)S(1)}, f32[4,128,128]{2,1,0:T(8,128)S(1)}, s32[]{:T(128)}, /*i...) while((s32[]{:T(128)}, f32[4,128,128]{2,0,1:T(4,128)S(1)}, ...), condition=%wide.region_1.2_spmd.clone, body=%wide.region_0.1_spmd.clone.sunk | while | flops 415367424 | bytes 6292374 | solution.py:92
  96.9 8.2 %collective-permute-start.1 = (f32[4,128,128]{2,1,0:T(8,128)S(1)}, f32[4,128,128]{2,1,0:T(8,128)S(1)}, u32[]{:S(2)}, u32[]{:S(2)}) collective-permute-start(f32[4,128,128]{2,1,0:T(8,128)S(1)} %copy.54), channel_id=1, source_target_pairs={{16,0},{32,16},{48,32},{64,48},{80,64},{96,80},{112,96},{128,112},... | collective-permute-start | bytes 786440 | tf_op jit(solution)/shard_map/while/body/eval_jaxpr/ppermute | solution.py:15
  111.9 4.4 collective-permute-start.1
  123.2 4.4 collective-permute-start.1
  134.7 4.4 collective-permute-start.1
  142.4 6.1 %collective-permute-start = (f32[4,128,128]{2,1,0:T(8,128)S(1)}, f32[4,128,128]{2,1,0:T(8,128)S(1)}, u32[]{:S(2)}, u32[]{:S(2)}) collective-permute-start(f32[4,128,128]{2,1,0:T(8,128)S(1)} %bitcast.164), channel_id=1, source_target_pairs={{1,0},{2,1},{3,2},{4,3},{5,4},{6,5},{7,6},{8,7},{9,8},{10,9},{11,1... | collective-permute-start | bytes 786440 | tf_op jit(solution)/shard_map/while/body/eval_jaxpr/ppermute | solution.py:15
  148.6 4.4 collective-permute-start.1
  156.3 6.1 %collective-permute-start = (f32[4,128,128]{2,1,0:T(8,128)S(1)}, f32[4,128,128]{2,1,0:T(8,128)S(1)}, u32[]{:S(2)}, u32[]{:S(2)}) collective-permute-start(f32[4,128,128]{2,1,0:T(8,128)S(1)} %bitcast.164), channel_id=1, source_target_pairs={{1,0},{2,1},{3,2},{4,3},{5,4},{6,5},{7,6},{8,7},{9,8},{10,9},{11,1... | collective-permute-start | bytes 786440 | tf_op jit(solution)/shard_map/while/body/eval_jaxpr/ppermute | solution.py:15
  162.4 4.4 collective-permute-start.1
  170.1 5.2 collective-permute-start
  175.3 4.4 collective-permute-start.1
  186.8 4.4 collective-permute-start.1
  194.5 5.0 collective-permute-start
  199.5 4.4 collective-permute-start.1
  207.2 6.1 %collective-permute-start = (f32[4,128,128]{2,1,0:T(8,128)S(1)}, f32[4,128,128]{2,1,0:T(8,128)S(1)}, u32[]{:S(2)}, u32[]{:S(2)}) collective-permute-start(f32[4,128,128]{2,1,0:T(8,128)S(1)} %bitcast.164), channel_id=1, source_target_pairs={{1,0},{2,1},{3,2},{4,3},{5,4},{6,5},{7,6},{8,7},{9,8},{10,9},{11,1... | collective-permute-start | bytes 786440 | tf_op jit(solution)/shard_map/while/body/eval_jaxpr/ppermute | solution.py:15
  213.3 4.4 collective-permute-start.1
  221.0 5.2 collective-permute-start
  226.3 4.4 collective-permute-start.1
  237.7 4.4 collective-permute-start.1
  245.4 5.0 collective-permute-start
  250.4 4.4 collective-permute-start.1
  258.1 6.1 %collective-permute-start = (f32[4,128,128]{2,1,0:T(8,128)S(1)}, f32[4,128,128]{2,1,0:T(8,128)S(1)}, u32[]{:S(2)}, u32[]{:S(2)}) collective-permute-start(f32[4,128,128]{2,1,0:T(8,128)S(1)} %bitcast.164), channel_id=1, source_target_pairs={{1,0},{2,1},{3,2},{4,3},{5,4},{6,5},{7,6},{8,7},{9,8},{10,9},{11,1... | collective-permute-start | bytes 786440 | tf_op jit(solution)/shard_map/while/body/eval_jaxpr/ppermute | solution.py:15
  264.3 4.4 collective-permute-start.1
  272.0 5.2 collective-permute-start
  277.2 4.4 collective-permute-start.1
  288.6 4.4 collective-permute-start.1
  296.4 5.2 collective-permute-start.12
  302.7 13.8 %collective-permute-start.13 = (f32[1,4,128,128]{3,2,1,0:T(8,128)S(1)}, f32[1,4,128,128]{3,2,1,0:T(8,128)S(1)}, u32[]{:S(2)}, u32[]{:S(2)}) collective-permute-start(f32[1,4,128,128]{3,2,1,0:T(8,128)S(1)} %broadcast_select_fusion.4), channel_id=1, source_target_pairs={{2,0},{3,1},{4,2},{5,3},{6,4},{7,5},{8,6},{9,7},{10,8},{11,9},{12,... | collective-permute-start | bytes 786440 | tf_op jit(solution)/shard_map/ppermute | solution.py:15
  321.5 6.3 %collective-permute-done.14 = f32[1,4,128,128]{3,2,1,0:T(8,128)S(1)} collective-permute-done((f32[1,4,128,128]{3,2,1,0:T(8,128)S(1)}, f32[1,4,128,128]{3,2,1,0:T(8,128)S(1)}, u32[]{:S(2)}, u32[]{:S(2)}) %collective-permute-start.14) | collective-permute-done | bytes 262176 | tf_op jit(solution)/shard_map/ppermute | solution.py:15
  328.3 8.7 %collective-permute-done.15 = f32[1,4,128,128]{3,2,1,0:T(8,128)S(1)} collective-permute-done((f32[1,4,128,128]{3,2,1,0:T(8,128)S(1)}, f32[1,4,128,128]{3,2,1,0:T(8,128)S(1)}, u32[]{:S(2)}, u32[]{:S(2)}) %collective-permute-start.15) | collective-permute-done | bytes 262176 | tf_op jit(solution)/shard_map/ppermute | solution.py:15
  337.1 198.0 %while.43 = (s32[]{:T(128)}, f32[4,128,128]{2,0,1:T(4,128)S(1)}, f32[1,4,128,128]{3,2,1,0:T(8,128)S(1)}, f32[4,128,128]{2,1,0:T(8,128)S(1)}, s32[]{:T(128)}, /*i...) while((s32[]{:T(128)}, f32[4,128,128]{2,0,1:T(4,128)S(1)}, ...), condition=%wide.region_3.4_spmd.clone, body=%wide.region_2.3_spmd.clone.sunk | while | flops 415367424 | bytes 6292374 | solution.py:92
  344.5 10.5 %collective-permute-start.2 = (f32[4,128,128]{2,1,0:T(8,128)S(1)}, f32[4,128,128]{2,1,0:T(8,128)S(1)}, u32[]{:S(2)}, u32[]{:S(2)}) collective-permute-start(f32[4,128,128]{2,1,0:T(8,128)S(1)} %bitcast.165), channel_id=1, source_target_pairs={{1,0},{2,1},{3,2},{4,3},{5,4},{6,5},{7,6},{8,7},{9,8},{10,9},{11,1... | collective-permute-start | bytes 786440 | tf_op jit(solution)/shard_map/while/body/eval_jaxpr/ppermute | solution.py:15
  360.3 6.3 %collective-permute-start.2 = (f32[4,128,128]{2,1,0:T(8,128)S(1)}, f32[4,128,128]{2,1,0:T(8,128)S(1)}, u32[]{:S(2)}, u32[]{:S(2)}) collective-permute-start(f32[4,128,128]{2,1,0:T(8,128)S(1)} %bitcast.165), channel_id=1, source_target_pairs={{1,0},{2,1},{3,2},{4,3},{5,4},{6,5},{7,6},{8,7},{9,8},{10,9},{11,1... | collective-permute-start | bytes 786440 | tf_op jit(solution)/shard_map/while/body/eval_jaxpr/ppermute | solution.py:15
  372.0 4.7 collective-permute-start.2
  383.6 5.1 collective-permute-start.2
  388.6 4.4 collective-permute-start.3
  400.0 4.4 collective-permute-start.3
  407.8 4.5 collective-permute-start.2
  412.3 4.4 collective-permute-start.3
  420.0 5.4 %collective-permute-start.2 = (f32[4,128,128]{2,1,0:T(8,128)S(1)}, f32[4,128,128]{2,1,0:T(8,128)S(1)}, u32[]{:S(2)}, u32[]{:S(2)}) collective-permute-start(f32[4,128,128]{2,1,0:T(8,128)S(1)} %bitcast.165), channel_id=1, source_target_pairs={{1,0},{2,1},{3,2},{4,3},{5,4},{6,5},{7,6},{8,7},{9,8},{10,9},{11,1... | collective-permute-start | bytes 786440 | tf_op jit(solution)/shard_map/while/body/eval_jaxpr/ppermute | solution.py:15
  425.4 4.4 collective-permute-start.3
  433.2 5.9 %collective-permute-start.2 = (f32[4,128,128]{2,1,0:T(8,128)S(1)}, f32[4,128,128]{2,1,0:T(8,128)S(1)}, u32[]{:S(2)}, u32[]{:S(2)}) collective-permute-start(f32[4,128,128]{2,1,0:T(8,128)S(1)} %bitcast.165), channel_id=1, source_target_pairs={{1,0},{2,1},{3,2},{4,3},{5,4},{6,5},{7,6},{8,7},{9,8},{10,9},{11,1... | collective-permute-start | bytes 786440 | tf_op jit(solution)/shard_map/while/body/eval_jaxpr/ppermute | solution.py:15
  439.1 4.4 collective-permute-start.3
  446.8 4.4 collective-permute-start.2
  451.2 4.4 collective-permute-start.3
  459.0 4.3 collective-permute-start.2
  463.2 4.4 collective-permute-start.3
  471.0 5.4 %collective-permute-start.2 = (f32[4,128,128]{2,1,0:T(8,128)S(1)}, f32[4,128,128]{2,1,0:T(8,128)S(1)}, u32[]{:S(2)}, u32[]{:S(2)}) collective-permute-start(f32[4,128,128]{2,1,0:T(8,128)S(1)} %bitcast.165), channel_id=1, source_target_pairs={{1,0},{2,1},{3,2},{4,3},{5,4},{6,5},{7,6},{8,7},{9,8},{10,9},{11,1... | collective-permute-start | bytes 786440 | tf_op jit(solution)/shard_map/while/body/eval_jaxpr/ppermute | solution.py:15
  476.4 4.4 collective-permute-start.3
  484.1 5.9 %collective-permute-start.2 = (f32[4,128,128]{2,1,0:T(8,128)S(1)}, f32[4,128,128]{2,1,0:T(8,128)S(1)}, u32[]{:S(2)}, u32[]{:S(2)}) collective-permute-start(f32[4,128,128]{2,1,0:T(8,128)S(1)} %bitcast.165), channel_id=1, source_target_pairs={{1,0},{2,1},{3,2},{4,3},{5,4},{6,5},{7,6},{8,7},{9,8},{10,9},{11,1... | collective-permute-start | bytes 786440 | tf_op jit(solution)/shard_map/while/body/eval_jaxpr/ppermute | solution.py:15
  490.0 4.4 collective-permute-start.3
  497.8 4.4 collective-permute-start.2
  502.2 4.4 collective-permute-start.3
  514.2 4.4 collective-permute-start.3
  521.9 5.4 %collective-permute-start.2 = (f32[4,128,128]{2,1,0:T(8,128)S(1)}, f32[4,128,128]{2,1,0:T(8,128)S(1)}, u32[]{:S(2)}, u32[]{:S(2)}) collective-permute-start(f32[4,128,128]{2,1,0:T(8,128)S(1)} %bitcast.165), channel_id=1, source_target_pairs={{1,0},{2,1},{3,2},{4,3},{5,4},{6,5},{7,6},{8,7},{9,8},{10,9},{11,1... | collective-permute-start | bytes 786440 | tf_op jit(solution)/shard_map/while/body/eval_jaxpr/ppermute | solution.py:15
  527.3 4.4 collective-permute-start.3
  (507 shorter events, 171.0 us)
Async XLA Ops:
  49.1 11.3 %collective-permute-start.8 = (f32[4,128,128]{2,1,0:T(8,128)S(1)}, f32[4,128,128]{2,1,0:T(8,128)S(1)}, u32[]{:S(2)}, u32[]{:S(2)}) collective-permute-start(f32[4,128,128]{2,1,0:T(8,128)S(1)} %get-tuple-element.699), channel_id=1, source_target_pairs={{16,0},{32,16},{48,32},{64,48},{80,64},{96,80},{112,96},{128,112},... | collective-permute-start | bytes 786440 | tf_op jit(solution)/shard_map/ppermute | solution.py:15
  62.6 8.6 %collective-permute-start.5 = (f32[1,4,128,128]{3,2,1,0:T(8,128)S(1)}, f32[1,4,128,128]{3,2,1,0:T(8,128)S(1)}, u32[]{:S(2)}, u32[]{:S(2)}) collective-permute-start(f32[1,4,128,128]{3,2,1,0:T(8,128)S(1)} %broadcast_select_fusion.5), channel_id=1, source_target_pairs={{2,0},{3,1},{4,2},{5,3},{6,4},{7,5},{8,6},{9,7},{10,8},{11,9},{12,... | collective-permute-start | bytes 786440 | tf_op jit(solution)/shard_map/ppermute | solution.py:15
  67.3 10.9 %collective-permute-start.10 = (f32[4,128,128]{2,1,0:T(8,128)S(1)}, f32[4,128,128]{2,1,0:T(8,128)S(1)}, u32[]{:S(2)}, u32[]{:S(2)}) collective-permute-start(f32[4,128,128]{2,1,0:T(8,128)S(1)} %broadcast_select_fusion.1), channel_id=1, source_target_pairs={{64,0},{80,16},{96,32},{112,48},{128,64},{144,80},{160,96},{176,11... | collective-permute-start | bytes 786440 | tf_op jit(solution)/shard_map/ppermute | solution.py:15
  71.3 11.8 %collective-permute-start.6 = (f32[1,4,128,128]{3,2,1,0:T(8,128)S(1)}, f32[1,4,128,128]{3,2,1,0:T(8,128)S(1)}, u32[]{:S(2)}, u32[]{:S(2)}) collective-permute-start(f32[1,4,128,128]{3,2,1,0:T(8,128)S(1)} %broadcast_select_fusion.7), channel_id=1, source_target_pairs={{4,0},{5,1},{6,2},{7,3},{8,4},{9,5},{10,6},{11,7},{12,8},{13,9},{1... | collective-permute-start | bytes 786440 | tf_op jit(solution)/shard_map/ppermute | solution.py:15
  78.3 16.2 %collective-permute-start.11 = (f32[4,128,128]{2,1,0:T(8,128)S(1)}, f32[4,128,128]{2,1,0:T(8,128)S(1)}, u32[]{:S(2)}, u32[]{:S(2)}) collective-permute-start(f32[4,128,128]{2,1,0:T(8,128)S(1)} %broadcast_select_fusion.2), channel_id=1, source_target_pairs={{128,0},{144,16},{160,32},{176,48},{192,64},{208,80},{224,96},{240... | collective-permute-start | bytes 786440 | tf_op jit(solution)/shard_map/ppermute | solution.py:15
  83.1 11.4 %collective-permute-start.7 = (f32[1,4,128,128]{3,2,1,0:T(8,128)S(1)}, f32[1,4,128,128]{3,2,1,0:T(8,128)S(1)}, u32[]{:S(2)}, u32[]{:S(2)}) collective-permute-start(f32[1,4,128,128]{3,2,1,0:T(8,128)S(1)} %broadcast_select_fusion.9), channel_id=1, source_target_pairs={{8,0},{9,1},{10,2},{11,3},{12,4},{13,5},{14,6},{15,7},{0,8},{1,9},... | collective-permute-start | bytes 786440 | tf_op jit(solution)/shard_map/ppermute | solution.py:15
  94.6 13.5 %collective-permute-start = (f32[4,128,128]{2,1,0:T(8,128)S(1)}, f32[4,128,128]{2,1,0:T(8,128)S(1)}, u32[]{:S(2)}, u32[]{:S(2)}) collective-permute-start(f32[4,128,128]{2,1,0:T(8,128)S(1)} %bitcast.164), channel_id=1, source_target_pairs={{1,0},{2,1},{3,2},{4,3},{5,4},{6,5},{7,6},{8,7},{9,8},{10,9},{11,1... | collective-permute-start | bytes 786440 | tf_op jit(solution)/shard_map/while/body/eval_jaxpr/ppermute | solution.py:15
  96.9 11.6 %collective-permute-start.1 = (f32[4,128,128]{2,1,0:T(8,128)S(1)}, f32[4,128,128]{2,1,0:T(8,128)S(1)}, u32[]{:S(2)}, u32[]{:S(2)}) collective-permute-start(f32[4,128,128]{2,1,0:T(8,128)S(1)} %copy.54), channel_id=1, source_target_pairs={{16,0},{32,16},{48,32},{64,48},{80,64},{96,80},{112,96},{128,112},... | collective-permute-start | bytes 786440 | tf_op jit(solution)/shard_map/while/body/eval_jaxpr/ppermute | solution.py:15
  108.4 10.9 %collective-permute-start = (f32[4,128,128]{2,1,0:T(8,128)S(1)}, f32[4,128,128]{2,1,0:T(8,128)S(1)}, u32[]{:S(2)}, u32[]{:S(2)}) collective-permute-start(f32[4,128,128]{2,1,0:T(8,128)S(1)} %bitcast.164), channel_id=1, source_target_pairs={{1,0},{2,1},{3,2},{4,3},{5,4},{6,5},{7,6},{8,7},{9,8},{10,9},{11,1... | collective-permute-start | bytes 786440 | tf_op jit(solution)/shard_map/while/body/eval_jaxpr/ppermute | solution.py:15
  111.9 7.7 %collective-permute-start.1 = (f32[4,128,128]{2,1,0:T(8,128)S(1)}, f32[4,128,128]{2,1,0:T(8,128)S(1)}, u32[]{:S(2)}, u32[]{:S(2)}) collective-permute-start(f32[4,128,128]{2,1,0:T(8,128)S(1)} %copy.54), channel_id=1, source_target_pairs={{16,0},{32,16},{48,32},{64,48},{80,64},{96,80},{112,96},{128,112},... | collective-permute-start | bytes 786440 | tf_op jit(solution)/shard_map/while/body/eval_jaxpr/ppermute | solution.py:15
  119.6 11.0 %collective-permute-start = (f32[4,128,128]{2,1,0:T(8,128)S(1)}, f32[4,128,128]{2,1,0:T(8,128)S(1)}, u32[]{:S(2)}, u32[]{:S(2)}) collective-permute-start(f32[4,128,128]{2,1,0:T(8,128)S(1)} %bitcast.164), channel_id=1, source_target_pairs={{1,0},{2,1},{3,2},{4,3},{5,4},{6,5},{7,6},{8,7},{9,8},{10,9},{11,1... | collective-permute-start | bytes 786440 | tf_op jit(solution)/shard_map/while/body/eval_jaxpr/ppermute | solution.py:15
  123.2 7.7 %collective-permute-start.1 = (f32[4,128,128]{2,1,0:T(8,128)S(1)}, f32[4,128,128]{2,1,0:T(8,128)S(1)}, u32[]{:S(2)}, u32[]{:S(2)}) collective-permute-start(f32[4,128,128]{2,1,0:T(8,128)S(1)} %copy.54), channel_id=1, source_target_pairs={{16,0},{32,16},{48,32},{64,48},{80,64},{96,80},{112,96},{128,112},... | collective-permute-start | bytes 786440 | tf_op jit(solution)/shard_map/while/body/eval_jaxpr/ppermute | solution.py:15
  130.9 11.3 %collective-permute-start = (f32[4,128,128]{2,1,0:T(8,128)S(1)}, f32[4,128,128]{2,1,0:T(8,128)S(1)}, u32[]{:S(2)}, u32[]{:S(2)}) collective-permute-start(f32[4,128,128]{2,1,0:T(8,128)S(1)} %bitcast.164), channel_id=1, source_target_pairs={{1,0},{2,1},{3,2},{4,3},{5,4},{6,5},{7,6},{8,7},{9,8},{10,9},{11,1... | collective-permute-start | bytes 786440 | tf_op jit(solution)/shard_map/while/body/eval_jaxpr/ppermute | solution.py:15
  134.7 7.7 %collective-permute-start.1 = (f32[4,128,128]{2,1,0:T(8,128)S(1)}, f32[4,128,128]{2,1,0:T(8,128)S(1)}, u32[]{:S(2)}, u32[]{:S(2)}) collective-permute-start(f32[4,128,128]{2,1,0:T(8,128)S(1)} %copy.54), channel_id=1, source_target_pairs={{16,0},{32,16},{48,32},{64,48},{80,64},{96,80},{112,96},{128,112},... | collective-permute-start | bytes 786440 | tf_op jit(solution)/shard_map/while/body/eval_jaxpr/ppermute | solution.py:15
  142.4 13.6 %collective-permute-start = (f32[4,128,128]{2,1,0:T(8,128)S(1)}, f32[4,128,128]{2,1,0:T(8,128)S(1)}, u32[]{:S(2)}, u32[]{:S(2)}) collective-permute-start(f32[4,128,128]{2,1,0:T(8,128)S(1)} %bitcast.164), channel_id=1, source_target_pairs={{1,0},{2,1},{3,2},{4,3},{5,4},{6,5},{7,6},{8,7},{9,8},{10,9},{11,1... | collective-permute-start | bytes 786440 | tf_op jit(solution)/shard_map/while/body/eval_jaxpr/ppermute | solution.py:15
  148.6 7.7 %collective-permute-start.1 = (f32[4,128,128]{2,1,0:T(8,128)S(1)}, f32[4,128,128]{2,1,0:T(8,128)S(1)}, u32[]{:S(2)}, u32[]{:S(2)}) collective-permute-start(f32[4,128,128]{2,1,0:T(8,128)S(1)} %copy.54), channel_id=1, source_target_pairs={{16,0},{32,16},{48,32},{64,48},{80,64},{96,80},{112,96},{128,112},... | collective-permute-start | bytes 786440 | tf_op jit(solution)/shard_map/while/body/eval_jaxpr/ppermute | solution.py:15
  156.3 13.6 %collective-permute-start = (f32[4,128,128]{2,1,0:T(8,128)S(1)}, f32[4,128,128]{2,1,0:T(8,128)S(1)}, u32[]{:S(2)}, u32[]{:S(2)}) collective-permute-start(f32[4,128,128]{2,1,0:T(8,128)S(1)} %bitcast.164), channel_id=1, source_target_pairs={{1,0},{2,1},{3,2},{4,3},{5,4},{6,5},{7,6},{8,7},{9,8},{10,9},{11,1... | collective-permute-start | bytes 786440 | tf_op jit(solution)/shard_map/while/body/eval_jaxpr/ppermute | solution.py:15
  162.4 7.7 %collective-permute-start.1 = (f32[4,128,128]{2,1,0:T(8,128)S(1)}, f32[4,128,128]{2,1,0:T(8,128)S(1)}, u32[]{:S(2)}, u32[]{:S(2)}) collective-permute-start(f32[4,128,128]{2,1,0:T(8,128)S(1)} %copy.54), channel_id=1, source_target_pairs={{16,0},{32,16},{48,32},{64,48},{80,64},{96,80},{112,96},{128,112},... | collective-permute-start | bytes 786440 | tf_op jit(solution)/shard_map/while/body/eval_jaxpr/ppermute | solution.py:15
  170.1 12.6 %collective-permute-start = (f32[4,128,128]{2,1,0:T(8,128)S(1)}, f32[4,128,128]{2,1,0:T(8,128)S(1)}, u32[]{:S(2)}, u32[]{:S(2)}) collective-permute-start(f32[4,128,128]{2,1,0:T(8,128)S(1)} %bitcast.164), channel_id=1, source_target_pairs={{1,0},{2,1},{3,2},{4,3},{5,4},{6,5},{7,6},{8,7},{9,8},{10,9},{11,1... | collective-permute-start | bytes 786440 | tf_op jit(solution)/shard_map/while/body/eval_jaxpr/ppermute | solution.py:15
  175.3 7.7 %collective-permute-start.1 = (f32[4,128,128]{2,1,0:T(8,128)S(1)}, f32[4,128,128]{2,1,0:T(8,128)S(1)}, u32[]{:S(2)}, u32[]{:S(2)}) collective-permute-start(f32[4,128,128]{2,1,0:T(8,128)S(1)} %copy.54), channel_id=1, source_target_pairs={{16,0},{32,16},{48,32},{64,48},{80,64},{96,80},{112,96},{128,112},... | collective-permute-start | bytes 786440 | tf_op jit(solution)/shard_map/while/body/eval_jaxpr/ppermute | solution.py:15
  183.0 11.2 %collective-permute-start = (f32[4,128,128]{2,1,0:T(8,128)S(1)}, f32[4,128,128]{2,1,0:T(8,128)S(1)}, u32[]{:S(2)}, u32[]{:S(2)}) collective-permute-start(f32[4,128,128]{2,1,0:T(8,128)S(1)} %bitcast.164), channel_id=1, source_target_pairs={{1,0},{2,1},{3,2},{4,3},{5,4},{6,5},{7,6},{8,7},{9,8},{10,9},{11,1... | collective-permute-start | bytes 786440 | tf_op jit(solution)/shard_map/while/body/eval_jaxpr/ppermute | solution.py:15
  186.8 7.7 %collective-permute-start.1 = (f32[4,128,128]{2,1,0:T(8,128)S(1)}, f32[4,128,128]{2,1,0:T(8,128)S(1)}, u32[]{:S(2)}, u32[]{:S(2)}) collective-permute-start(f32[4,128,128]{2,1,0:T(8,128)S(1)} %copy.54), channel_id=1, source_target_pairs={{16,0},{32,16},{48,32},{64,48},{80,64},{96,80},{112,96},{128,112},... | collective-permute-start | bytes 786440 | tf_op jit(solution)/shard_map/while/body/eval_jaxpr/ppermute | solution.py:15
  194.5 12.4 %collective-permute-start = (f32[4,128,128]{2,1,0:T(8,128)S(1)}, f32[4,128,128]{2,1,0:T(8,128)S(1)}, u32[]{:S(2)}, u32[]{:S(2)}) collective-permute-start(f32[4,128,128]{2,1,0:T(8,128)S(1)} %bitcast.164), channel_id=1, source_target_pairs={{1,0},{2,1},{3,2},{4,3},{5,4},{6,5},{7,6},{8,7},{9,8},{10,9},{11,1... | collective-permute-start | bytes 786440 | tf_op jit(solution)/shard_map/while/body/eval_jaxpr/ppermute | solution.py:15
  199.5 7.7 %collective-permute-start.1 = (f32[4,128,128]{2,1,0:T(8,128)S(1)}, f32[4,128,128]{2,1,0:T(8,128)S(1)}, u32[]{:S(2)}, u32[]{:S(2)}) collective-permute-start(f32[4,128,128]{2,1,0:T(8,128)S(1)} %copy.54), channel_id=1, source_target_pairs={{16,0},{32,16},{48,32},{64,48},{80,64},{96,80},{112,96},{128,112},... | collective-permute-start | bytes 786440 | tf_op jit(solution)/shard_map/while/body/eval_jaxpr/ppermute | solution.py:15
  207.2 13.6 %collective-permute-start = (f32[4,128,128]{2,1,0:T(8,128)S(1)}, f32[4,128,128]{2,1,0:T(8,128)S(1)}, u32[]{:S(2)}, u32[]{:S(2)}) collective-permute-start(f32[4,128,128]{2,1,0:T(8,128)S(1)} %bitcast.164), channel_id=1, source_target_pairs={{1,0},{2,1},{3,2},{4,3},{5,4},{6,5},{7,6},{8,7},{9,8},{10,9},{11,1... | collective-permute-start | bytes 786440 | tf_op jit(solution)/shard_map/while/body/eval_jaxpr/ppermute | solution.py:15
  213.3 7.7 %collective-permute-start.1 = (f32[4,128,128]{2,1,0:T(8,128)S(1)}, f32[4,128,128]{2,1,0:T(8,128)S(1)}, u32[]{:S(2)}, u32[]{:S(2)}) collective-permute-start(f32[4,128,128]{2,1,0:T(8,128)S(1)} %copy.54), channel_id=1, source_target_pairs={{16,0},{32,16},{48,32},{64,48},{80,64},{96,80},{112,96},{128,112},... | collective-permute-start | bytes 786440 | tf_op jit(solution)/shard_map/while/body/eval_jaxpr/ppermute | solution.py:15
  221.0 12.6 %collective-permute-start = (f32[4,128,128]{2,1,0:T(8,128)S(1)}, f32[4,128,128]{2,1,0:T(8,128)S(1)}, u32[]{:S(2)}, u32[]{:S(2)}) collective-permute-start(f32[4,128,128]{2,1,0:T(8,128)S(1)} %bitcast.164), channel_id=1, source_target_pairs={{1,0},{2,1},{3,2},{4,3},{5,4},{6,5},{7,6},{8,7},{9,8},{10,9},{11,1... | collective-permute-start | bytes 786440 | tf_op jit(solution)/shard_map/while/body/eval_jaxpr/ppermute | solution.py:15
  226.3 7.7 %collective-permute-start.1 = (f32[4,128,128]{2,1,0:T(8,128)S(1)}, f32[4,128,128]{2,1,0:T(8,128)S(1)}, u32[]{:S(2)}, u32[]{:S(2)}) collective-permute-start(f32[4,128,128]{2,1,0:T(8,128)S(1)} %copy.54), channel_id=1, source_target_pairs={{16,0},{32,16},{48,32},{64,48},{80,64},{96,80},{112,96},{128,112},... | collective-permute-start | bytes 786440 | tf_op jit(solution)/shard_map/while/body/eval_jaxpr/ppermute | solution.py:15
  234.0 11.2 %collective-permute-start = (f32[4,128,128]{2,1,0:T(8,128)S(1)}, f32[4,128,128]{2,1,0:T(8,128)S(1)}, u32[]{:S(2)}, u32[]{:S(2)}) collective-permute-start(f32[4,128,128]{2,1,0:T(8,128)S(1)} %bitcast.164), channel_id=1, source_target_pairs={{1,0},{2,1},{3,2},{4,3},{5,4},{6,5},{7,6},{8,7},{9,8},{10,9},{11,1... | collective-permute-start | bytes 786440 | tf_op jit(solution)/shard_map/while/body/eval_jaxpr/ppermute | solution.py:15
  237.7 7.7 %collective-permute-start.1 = (f32[4,128,128]{2,1,0:T(8,128)S(1)}, f32[4,128,128]{2,1,0:T(8,128)S(1)}, u32[]{:S(2)}, u32[]{:S(2)}) collective-permute-start(f32[4,128,128]{2,1,0:T(8,128)S(1)} %copy.54), channel_id=1, source_target_pairs={{16,0},{32,16},{48,32},{64,48},{80,64},{96,80},{112,96},{128,112},... | collective-permute-start | bytes 786440 | tf_op jit(solution)/shard_map/while/body/eval_jaxpr/ppermute | solution.py:15
  245.4 12.4 %collective-permute-start = (f32[4,128,128]{2,1,0:T(8,128)S(1)}, f32[4,128,128]{2,1,0:T(8,128)S(1)}, u32[]{:S(2)}, u32[]{:S(2)}) collective-permute-start(f32[4,128,128]{2,1,0:T(8,128)S(1)} %bitcast.164), channel_id=1, source_target_pairs={{1,0},{2,1},{3,2},{4,3},{5,4},{6,5},{7,6},{8,7},{9,8},{10,9},{11,1... | collective-permute-start | bytes 786440 | tf_op jit(solution)/shard_map/while/body/eval_jaxpr/ppermute | solution.py:15
  250.4 7.7 %collective-permute-start.1 = (f32[4,128,128]{2,1,0:T(8,128)S(1)}, f32[4,128,128]{2,1,0:T(8,128)S(1)}, u32[]{:S(2)}, u32[]{:S(2)}) collective-permute-start(f32[4,128,128]{2,1,0:T(8,128)S(1)} %copy.54), channel_id=1, source_target_pairs={{16,0},{32,16},{48,32},{64,48},{80,64},{96,80},{112,96},{128,112},... | collective-permute-start | bytes 786440 | tf_op jit(solution)/shard_map/while/body/eval_jaxpr/ppermute | solution.py:15
  258.1 13.6 %collective-permute-start = (f32[4,128,128]{2,1,0:T(8,128)S(1)}, f32[4,128,128]{2,1,0:T(8,128)S(1)}, u32[]{:S(2)}, u32[]{:S(2)}) collective-permute-start(f32[4,128,128]{2,1,0:T(8,128)S(1)} %bitcast.164), channel_id=1, source_target_pairs={{1,0},{2,1},{3,2},{4,3},{5,4},{6,5},{7,6},{8,7},{9,8},{10,9},{11,1... | collective-permute-start | bytes 786440 | tf_op jit(solution)/shard_map/while/body/eval_jaxpr/ppermute | solution.py:15
  264.3 7.7 %collective-permute-start.1 = (f32[4,128,128]{2,1,0:T(8,128)S(1)}, f32[4,128,128]{2,1,0:T(8,128)S(1)}, u32[]{:S(2)}, u32[]{:S(2)}) collective-permute-start(f32[4,128,128]{2,1,0:T(8,128)S(1)} %copy.54), channel_id=1, source_target_pairs={{16,0},{32,16},{48,32},{64,48},{80,64},{96,80},{112,96},{128,112},... | collective-permute-start | bytes 786440 | tf_op jit(solution)/shard_map/while/body/eval_jaxpr/ppermute | solution.py:15
  272.0 12.6 %collective-permute-start = (f32[4,128,128]{2,1,0:T(8,128)S(1)}, f32[4,128,128]{2,1,0:T(8,128)S(1)}, u32[]{:S(2)}, u32[]{:S(2)}) collective-permute-start(f32[4,128,128]{2,1,0:T(8,128)S(1)} %bitcast.164), channel_id=1, source_target_pairs={{1,0},{2,1},{3,2},{4,3},{5,4},{6,5},{7,6},{8,7},{9,8},{10,9},{11,1... | collective-permute-start | bytes 786440 | tf_op jit(solution)/shard_map/while/body/eval_jaxpr/ppermute | solution.py:15
  277.2 7.7 %collective-permute-start.1 = (f32[4,128,128]{2,1,0:T(8,128)S(1)}, f32[4,128,128]{2,1,0:T(8,128)S(1)}, u32[]{:S(2)}, u32[]{:S(2)}) collective-permute-start(f32[4,128,128]{2,1,0:T(8,128)S(1)} %copy.54), channel_id=1, source_target_pairs={{16,0},{32,16},{48,32},{64,48},{80,64},{96,80},{112,96},{128,112},... | collective-permute-start | bytes 786440 | tf_op jit(solution)/shard_map/while/body/eval_jaxpr/ppermute | solution.py:15
  284.9 11.2 %collective-permute-start = (f32[4,128,128]{2,1,0:T(8,128)S(1)}, f32[4,128,128]{2,1,0:T(8,128)S(1)}, u32[]{:S(2)}, u32[]{:S(2)}) collective-permute-start(f32[4,128,128]{2,1,0:T(8,128)S(1)} %bitcast.164), channel_id=1, source_target_pairs={{1,0},{2,1},{3,2},{4,3},{5,4},{6,5},{7,6},{8,7},{9,8},{10,9},{11,1... | collective-permute-start | bytes 786440 | tf_op jit(solution)/shard_map/while/body/eval_jaxpr/ppermute | solution.py:15
  288.6 7.7 %collective-permute-start.1 = (f32[4,128,128]{2,1,0:T(8,128)S(1)}, f32[4,128,128]{2,1,0:T(8,128)S(1)}, u32[]{:S(2)}, u32[]{:S(2)}) collective-permute-start(f32[4,128,128]{2,1,0:T(8,128)S(1)} %copy.54), channel_id=1, source_target_pairs={{16,0},{32,16},{48,32},{64,48},{80,64},{96,80},{112,96},{128,112},... | collective-permute-start | bytes 786440 | tf_op jit(solution)/shard_map/while/body/eval_jaxpr/ppermute | solution.py:15
  302.7 17.1 %collective-permute-start.13 = (f32[1,4,128,128]{3,2,1,0:T(8,128)S(1)}, f32[1,4,128,128]{3,2,1,0:T(8,128)S(1)}, u32[]{:S(2)}, u32[]{:S(2)}) collective-permute-start(f32[1,4,128,128]{3,2,1,0:T(8,128)S(1)} %broadcast_select_fusion.4), channel_id=1, source_target_pairs={{2,0},{3,1},{4,2},{5,3},{6,4},{7,5},{8,6},{9,7},{10,8},{11,9},{12,... | collective-permute-start | bytes 786440 | tf_op jit(solution)/shard_map/ppermute | solution.py:15
  319.8 8.0 %collective-permute-start.14 = (f32[1,4,128,128]{3,2,1,0:T(8,128)S(1)}, f32[1,4,128,128]{3,2,1,0:T(8,128)S(1)}, u32[]{:S(2)}, u32[]{:S(2)}) collective-permute-start(f32[1,4,128,128]{3,2,1,0:T(8,128)S(1)} %broadcast_select_fusion.6), channel_id=1, source_target_pairs={{4,0},{5,1},{6,2},{7,3},{8,4},{9,5},{10,6},{11,7},{12,8},{13,9},{1... | collective-permute-start | bytes 786440 | tf_op jit(solution)/shard_map/ppermute | solution.py:15
  327.9 9.2 %collective-permute-start.15 = (f32[1,4,128,128]{3,2,1,0:T(8,128)S(1)}, f32[1,4,128,128]{3,2,1,0:T(8,128)S(1)}, u32[]{:S(2)}, u32[]{:S(2)}) collective-permute-start(f32[1,4,128,128]{3,2,1,0:T(8,128)S(1)} %broadcast_select_fusion.8), channel_id=1, source_target_pairs={{8,0},{9,1},{10,2},{11,3},{12,4},{13,5},{14,6},{15,7},{0,8},{1,9},... | collective-permute-start | bytes 786440 | tf_op jit(solution)/shard_map/ppermute | solution.py:15
  344.5 15.5 %collective-permute-start.2 = (f32[4,128,128]{2,1,0:T(8,128)S(1)}, f32[4,128,128]{2,1,0:T(8,128)S(1)}, u32[]{:S(2)}, u32[]{:S(2)}) collective-permute-start(f32[4,128,128]{2,1,0:T(8,128)S(1)} %bitcast.165), channel_id=1, source_target_pairs={{1,0},{2,1},{3,2},{4,3},{5,4},{6,5},{7,6},{8,7},{9,8},{10,9},{11,1... | collective-permute-start | bytes 786440 | tf_op jit(solution)/shard_map/while/body/eval_jaxpr/ppermute | solution.py:15
  360.3 11.3 %collective-permute-start.2 = (f32[4,128,128]{2,1,0:T(8,128)S(1)}, f32[4,128,128]{2,1,0:T(8,128)S(1)}, u32[]{:S(2)}, u32[]{:S(2)}) collective-permute-start(f32[4,128,128]{2,1,0:T(8,128)S(1)} %bitcast.165), channel_id=1, source_target_pairs={{1,0},{2,1},{3,2},{4,3},{5,4},{6,5},{7,6},{8,7},{9,8},{10,9},{11,1... | collective-permute-start | bytes 786440 | tf_op jit(solution)/shard_map/while/body/eval_jaxpr/ppermute | solution.py:15
  372.0 11.3 %collective-permute-start.2 = (f32[4,128,128]{2,1,0:T(8,128)S(1)}, f32[4,128,128]{2,1,0:T(8,128)S(1)}, u32[]{:S(2)}, u32[]{:S(2)}) collective-permute-start(f32[4,128,128]{2,1,0:T(8,128)S(1)} %bitcast.165), channel_id=1, source_target_pairs={{1,0},{2,1},{3,2},{4,3},{5,4},{6,5},{7,6},{8,7},{9,8},{10,9},{11,1... | collective-permute-start | bytes 786440 | tf_op jit(solution)/shard_map/while/body/eval_jaxpr/ppermute | solution.py:15
  383.6 12.5 %collective-permute-start.2 = (f32[4,128,128]{2,1,0:T(8,128)S(1)}, f32[4,128,128]{2,1,0:T(8,128)S(1)}, u32[]{:S(2)}, u32[]{:S(2)}) collective-permute-start(f32[4,128,128]{2,1,0:T(8,128)S(1)} %bitcast.165), channel_id=1, source_target_pairs={{1,0},{2,1},{3,2},{4,3},{5,4},{6,5},{7,6},{8,7},{9,8},{10,9},{11,1... | collective-permute-start | bytes 786440 | tf_op jit(solution)/shard_map/while/body/eval_jaxpr/ppermute | solution.py:15
  388.6 7.7 %collective-permute-start.3 = (f32[4,128,128]{2,1,0:T(8,128)S(1)}, f32[4,128,128]{2,1,0:T(8,128)S(1)}, u32[]{:S(2)}, u32[]{:S(2)}) collective-permute-start(f32[4,128,128]{2,1,0:T(8,128)S(1)} %copy.66), channel_id=1, source_target_pairs={{16,0},{32,16},{48,32},{64,48},{80,64},{96,80},{112,96},{128,112},... | collective-permute-start | bytes 786440 | tf_op jit(solution)/shard_map/while/body/eval_jaxpr/ppermute | solution.py:15
  396.4 11.1 %collective-permute-start.2 = (f32[4,128,128]{2,1,0:T(8,128)S(1)}, f32[4,128,128]{2,1,0:T(8,128)S(1)}, u32[]{:S(2)}, u32[]{:S(2)}) collective-permute-start(f32[4,128,128]{2,1,0:T(8,128)S(1)} %bitcast.165), channel_id=1, source_target_pairs={{1,0},{2,1},{3,2},{4,3},{5,4},{6,5},{7,6},{8,7},{9,8},{10,9},{11,1... | collective-permute-start | bytes 786440 | tf_op jit(solution)/shard_map/while/body/eval_jaxpr/ppermute | solution.py:15
  400.0 7.7 %collective-permute-start.3 = (f32[4,128,128]{2,1,0:T(8,128)S(1)}, f32[4,128,128]{2,1,0:T(8,128)S(1)}, u32[]{:S(2)}, u32[]{:S(2)}) collective-permute-start(f32[4,128,128]{2,1,0:T(8,128)S(1)} %copy.66), channel_id=1, source_target_pairs={{16,0},{32,16},{48,32},{64,48},{80,64},{96,80},{112,96},{128,112},... | collective-permute-start | bytes 786440 | tf_op jit(solution)/shard_map/while/body/eval_jaxpr/ppermute | solution.py:15
  407.8 12.0 %collective-permute-start.2 = (f32[4,128,128]{2,1,0:T(8,128)S(1)}, f32[4,128,128]{2,1,0:T(8,128)S(1)}, u32[]{:S(2)}, u32[]{:S(2)}) collective-permute-start(f32[4,128,128]{2,1,0:T(8,128)S(1)} %bitcast.165), channel_id=1, source_target_pairs={{1,0},{2,1},{3,2},{4,3},{5,4},{6,5},{7,6},{8,7},{9,8},{10,9},{11,1... | collective-permute-start | bytes 786440 | tf_op jit(solution)/shard_map/while/body/eval_jaxpr/ppermute | solution.py:15
  412.3 7.7 %collective-permute-start.3 = (f32[4,128,128]{2,1,0:T(8,128)S(1)}, f32[4,128,128]{2,1,0:T(8,128)S(1)}, u32[]{:S(2)}, u32[]{:S(2)}) collective-permute-start(f32[4,128,128]{2,1,0:T(8,128)S(1)} %copy.66), channel_id=1, source_target_pairs={{16,0},{32,16},{48,32},{64,48},{80,64},{96,80},{112,96},{128,112},... | collective-permute-start | bytes 786440 | tf_op jit(solution)/shard_map/while/body/eval_jaxpr/ppermute | solution.py:15
  420.0 12.9 %collective-permute-start.2 = (f32[4,128,128]{2,1,0:T(8,128)S(1)}, f32[4,128,128]{2,1,0:T(8,128)S(1)}, u32[]{:S(2)}, u32[]{:S(2)}) collective-permute-start(f32[4,128,128]{2,1,0:T(8,128)S(1)} %bitcast.165), channel_id=1, source_target_pairs={{1,0},{2,1},{3,2},{4,3},{5,4},{6,5},{7,6},{8,7},{9,8},{10,9},{11,1... | collective-permute-start | bytes 786440 | tf_op jit(solution)/shard_map/while/body/eval_jaxpr/ppermute | solution.py:15
  425.4 7.7 %collective-permute-start.3 = (f32[4,128,128]{2,1,0:T(8,128)S(1)}, f32[4,128,128]{2,1,0:T(8,128)S(1)}, u32[]{:S(2)}, u32[]{:S(2)}) collective-permute-start(f32[4,128,128]{2,1,0:T(8,128)S(1)} %copy.66), channel_id=1, source_target_pairs={{16,0},{32,16},{48,32},{64,48},{80,64},{96,80},{112,96},{128,112},... | collective-permute-start | bytes 786440 | tf_op jit(solution)/shard_map/while/body/eval_jaxpr/ppermute | solution.py:15
  433.2 13.4 %collective-permute-start.2 = (f32[4,128,128]{2,1,0:T(8,128)S(1)}, f32[4,128,128]{2,1,0:T(8,128)S(1)}, u32[]{:S(2)}, u32[]{:S(2)}) collective-permute-start(f32[4,128,128]{2,1,0:T(8,128)S(1)} %bitcast.165), channel_id=1, source_target_pairs={{1,0},{2,1},{3,2},{4,3},{5,4},{6,5},{7,6},{8,7},{9,8},{10,9},{11,1... | collective-permute-start | bytes 786440 | tf_op jit(solution)/shard_map/while/body/eval_jaxpr/ppermute | solution.py:15
  439.1 7.7 %collective-permute-start.3 = (f32[4,128,128]{2,1,0:T(8,128)S(1)}, f32[4,128,128]{2,1,0:T(8,128)S(1)}, u32[]{:S(2)}, u32[]{:S(2)}) collective-permute-start(f32[4,128,128]{2,1,0:T(8,128)S(1)} %copy.66), channel_id=1, source_target_pairs={{16,0},{32,16},{48,32},{64,48},{80,64},{96,80},{112,96},{128,112},... | collective-permute-start | bytes 786440 | tf_op jit(solution)/shard_map/while/body/eval_jaxpr/ppermute | solution.py:15
  446.8 11.9 %collective-permute-start.2 = (f32[4,128,128]{2,1,0:T(8,128)S(1)}, f32[4,128,128]{2,1,0:T(8,128)S(1)}, u32[]{:S(2)}, u32[]{:S(2)}) collective-permute-start(f32[4,128,128]{2,1,0:T(8,128)S(1)} %bitcast.165), channel_id=1, source_target_pairs={{1,0},{2,1},{3,2},{4,3},{5,4},{6,5},{7,6},{8,7},{9,8},{10,9},{11,1... | collective-permute-start | bytes 786440 | tf_op jit(solution)/shard_map/while/body/eval_jaxpr/ppermute | solution.py:15
  451.2 7.7 %collective-permute-start.3 = (f32[4,128,128]{2,1,0:T(8,128)S(1)}, f32[4,128,128]{2,1,0:T(8,128)S(1)}, u32[]{:S(2)}, u32[]{:S(2)}) collective-permute-start(f32[4,128,128]{2,1,0:T(8,128)S(1)} %copy.66), channel_id=1, source_target_pairs={{16,0},{32,16},{48,32},{64,48},{80,64},{96,80},{112,96},{128,112},... | collective-permute-start | bytes 786440 | tf_op jit(solution)/shard_map/while/body/eval_jaxpr/ppermute | solution.py:15
  459.0 11.7 %collective-permute-start.2 = (f32[4,128,128]{2,1,0:T(8,128)S(1)}, f32[4,128,128]{2,1,0:T(8,128)S(1)}, u32[]{:S(2)}, u32[]{:S(2)}) collective-permute-start(f32[4,128,128]{2,1,0:T(8,128)S(1)} %bitcast.165), channel_id=1, source_target_pairs={{1,0},{2,1},{3,2},{4,3},{5,4},{6,5},{7,6},{8,7},{9,8},{10,9},{11,1... | collective-permute-start | bytes 786440 | tf_op jit(solution)/shard_map/while/body/eval_jaxpr/ppermute | solution.py:15
  463.2 7.7 %collective-permute-start.3 = (f32[4,128,128]{2,1,0:T(8,128)S(1)}, f32[4,128,128]{2,1,0:T(8,128)S(1)}, u32[]{:S(2)}, u32[]{:S(2)}) collective-permute-start(f32[4,128,128]{2,1,0:T(8,128)S(1)} %copy.66), channel_id=1, source_target_pairs={{16,0},{32,16},{48,32},{64,48},{80,64},{96,80},{112,96},{128,112},... | collective-permute-start | bytes 786440 | tf_op jit(solution)/shard_map/while/body/eval_jaxpr/ppermute | solution.py:15
  471.0 12.9 %collective-permute-start.2 = (f32[4,128,128]{2,1,0:T(8,128)S(1)}, f32[4,128,128]{2,1,0:T(8,128)S(1)}, u32[]{:S(2)}, u32[]{:S(2)}) collective-permute-start(f32[4,128,128]{2,1,0:T(8,128)S(1)} %bitcast.165), channel_id=1, source_target_pairs={{1,0},{2,1},{3,2},{4,3},{5,4},{6,5},{7,6},{8,7},{9,8},{10,9},{11,1... | collective-permute-start | bytes 786440 | tf_op jit(solution)/shard_map/while/body/eval_jaxpr/ppermute | solution.py:15
  484.1 13.4 %collective-permute-start.2 = (f32[4,128,128]{2,1,0:T(8,128)S(1)}, f32[4,128,128]{2,1,0:T(8,128)S(1)}, u32[]{:S(2)}, u32[]{:S(2)}) collective-permute-start(f32[4,128,128]{2,1,0:T(8,128)S(1)} %bitcast.165), channel_id=1, source_target_pairs={{1,0},{2,1},{3,2},{4,3},{5,4},{6,5},{7,6},{8,7},{9,8},{10,9},{11,1... | collective-permute-start | bytes 786440 | tf_op jit(solution)/shard_map/while/body/eval_jaxpr/ppermute | solution.py:15
  497.8 11.9 %collective-permute-start.2 = (f32[4,128,128]{2,1,0:T(8,128)S(1)}, f32[4,128,128]{2,1,0:T(8,128)S(1)}, u32[]{:S(2)}, u32[]{:S(2)}) collective-permute-start(f32[4,128,128]{2,1,0:T(8,128)S(1)} %bitcast.165), channel_id=1, source_target_pairs={{1,0},{2,1},{3,2},{4,3},{5,4},{6,5},{7,6},{8,7},{9,8},{10,9},{11,1... | collective-permute-start | bytes 786440 | tf_op jit(solution)/shard_map/while/body/eval_jaxpr/ppermute | solution.py:15
  509.9 11.7 %collective-permute-start.2 = (f32[4,128,128]{2,1,0:T(8,128)S(1)}, f32[4,128,128]{2,1,0:T(8,128)S(1)}, u32[]{:S(2)}, u32[]{:S(2)}) collective-permute-start(f32[4,128,128]{2,1,0:T(8,128)S(1)} %bitcast.165), channel_id=1, source_target_pairs={{1,0},{2,1},{3,2},{4,3},{5,4},{6,5},{7,6},{8,7},{9,8},{10,9},{11,1... | collective-permute-start | bytes 786440 | tf_op jit(solution)/shard_map/while/body/eval_jaxpr/ppermute | solution.py:15
  514.2 7.7 %collective-permute-start.3 = (f32[4,128,128]{2,1,0:T(8,128)S(1)}, f32[4,128,128]{2,1,0:T(8,128)S(1)}, u32[]{:S(2)}, u32[]{:S(2)}) collective-permute-start(f32[4,128,128]{2,1,0:T(8,128)S(1)} %copy.66), channel_id=1, source_target_pairs={{16,0},{32,16},{48,32},{64,48},{80,64},{96,80},{112,96},{128,112},... | collective-permute-start | bytes 786440 | tf_op jit(solution)/shard_map/while/body/eval_jaxpr/ppermute | solution.py:15
  521.9 12.9 %collective-permute-start.2 = (f32[4,128,128]{2,1,0:T(8,128)S(1)}, f32[4,128,128]{2,1,0:T(8,128)S(1)}, u32[]{:S(2)}, u32[]{:S(2)}) collective-permute-start(f32[4,128,128]{2,1,0:T(8,128)S(1)} %bitcast.165), channel_id=1, source_target_pairs={{1,0},{2,1},{3,2},{4,3},{5,4},{6,5},{7,6},{8,7},{9,8},{10,9},{11,1... | collective-permute-start | bytes 786440 | tf_op jit(solution)/shard_map/while/body/eval_jaxpr/ppermute | solution.py:15
  (16 other events, 106.5 us)
where the time goes:
time: 541 us; the launch traced here: 536 us
  starting transfers between devices  337 us (62%)
  matrix products  89.2 us (16%)
  waiting for transfers between devices  49.4 us (9%)
  blocking collectives  45.2 us (8%)
  other arithmetic  9.19 us (2%)
    ppermute x76, starting transfers between devices, shifted(): return lax.ppermute(block, axis, route)  337 us
    dot_general x32, matrix products, accumulate(): return total + jnp.einsum('tab,axby->txy', weight, pairs, precision=highest)  57 us
    ppermute x76, waiting for transfers between devices, shifted(): return lax.ppermute(block, axis, route)  49.4 us
    dot_general x32, matrix products, accumulate(): jnp.einsum('axk,bky->axby', left_blocks, right_blocks, precision=highest)  31.1 us
    all_gather x1, blocking collectives, on_device(): lax.all_gather(band_vectors, 'col', axis=0, tiled=True)  26 us
    all_gather x1, blocking collectives, on_device(): lax.all_gather(band_blocks, 'col', axis=0, tiled=True)  19.3 us
  transfers between devices with their start and end apart: 76, of which 41 were waited for; matrix products, arithmetic and copies ran while one was open for 18% of the time, Pallas kernels for 0%

commit v1 on v0

v1 whole, which is shorter than its diff:
```python
import functools

import jax
import jax.numpy as jnp
from jax import lax
from jax.experimental import pallas as pl
from jax.experimental.pallas import tpu as pltpu
from jax.sharding import PartitionSpec as P

NB = 160
BS = 128
SLOTS = 4
MESH = pl.DeviceIdType.MESH

NZ = 8
NX = 4
HALF = 32
PACK = 12
TRIPLES = 20

highest = lax.Precision.HIGHEST


def shifted(block, axis, distance):
    devices = range(lax.axis_size(axis))
    route = [((i - distance) % len(devices), i) for i in devices]
    return lax.ppermute(block, axis, route)


def exchange_term(vectors, blocks, block_rows, block_cols):
    hit_row = (blocks[:, :, None] == block_rows[None, None, :]).astype(jnp.float32)
    hit_col = (blocks[:, :, None] == block_cols[None, None, :]).astype(jnp.float32)
    vec_row = jnp.einsum("bln,blx->bnx", hit_row, vectors, precision=highest)
    vec_col = jnp.einsum("bln,blx->bnx", hit_col, vectors, precision=highest)
    return -jnp.einsum("bnx,bny->nxy", vec_row, vec_col, precision=highest)


def tile_layout(layout, tile_row, tile_col):
    slots = layout.shape[1]
    start = (tile_row, jnp.int32(0), tile_col, jnp.int32(0))
    return lax.dynamic_slice(layout, start, (1, slots, 1, 2)).reshape(slots, 2)


def link_weights(targets, left_local, piece, right_local, tile_rows):
    row_target = targets[:, None, None, 0]
    col_target = targets[:, None, None, 1]
    row_left = left_local[None, :, None, 0]
    col_left = left_local[None, :, None, 1]
    row_right = right_local[None, None, :, 0]
    col_right = right_local[None, None, :, 1]
    keep = (row_left == row_target) & (col_left // tile_rows == piece)
    keep = keep & (col_left % tile_rows == row_right) & (col_right == col_target)
    return keep.astype(jnp.float32)


def accumulate(
    total, targets, left_blocks, left_local, piece, right_blocks, right_local, tile_rows
):
    weight = link_weights(targets, left_local, piece, right_local, tile_rows)
    pairs = jnp.einsum("axk,bky->axby", left_blocks, right_blocks, precision=highest)
    return total + jnp.einsum("tab,axby->txy", weight, pairs, precision=highest)


def align(block, axis, amount):
    for place in range((lax.axis_size(axis) - 1).bit_length()):
        moved = shifted(block, axis, -(1 << place))
        block = jnp.where(amount >> place & 1 == 1, moved, block)
    return block


def shifted_product(left, right, layout, targets, this_row, this_col, tile_rows):
    row_count = lax.axis_size("row")
    left = align(left, "col", this_row)

    def step_body(step, carry):
        total, left, right = carry
        source = (this_row + this_col + step) % row_count
        left_local = tile_layout(layout, this_row, source)
        right_local = tile_layout(layout, source, this_col)
        total = accumulate(
            total, targets, left, left_local, 0, right, right_local, tile_rows
        )
        left = shifted(left, "col", -1)
        right = shifted(right, "row", -1)
        return (total, left, right)

    total, left, right = lax.fori_loop(
        0, row_count, step_body, (jnp.zeros_like(left), left, right)
    )
    return (total, right)


def general(core_blocks, block_coords, band_vectors, band_blocks, spread):
    row_count = lax.axis_size("row")
    column_count = lax.axis_size("col")
    tile_rows = NB // row_count
    tile_columns = NB // column_count
    slots = core_blocks.shape[0]
    this_row = lax.axis_index("row")
    this_col = lax.axis_index("col")
    layout = block_coords.reshape(row_count, slots, column_count, 2)
    targets = tile_layout(layout, this_row, this_col)
    vectors, blocks = (
        lax.all_gather(band_vectors, "col", axis=0, tiled=True),
        lax.all_gather(band_blocks, "col", axis=0, tiled=True),
    )
    block_rows = this_row * tile_rows + targets[:, 0]
    block_cols = this_col * tile_columns + targets[:, 1]
    exchange = exchange_term(vectors, blocks, block_rows, block_cols)
    fock = core_blocks + exchange
    scaled = fock / spread
    right = align(scaled, "row", this_col)
    square, right = shifted_product(
        scaled, right, layout, targets, this_row, this_col, tile_rows
    )
    cube, right = shifted_product(
        square, right, layout, targets, this_row, this_col, tile_rows
    )
    return 1.5 * fock - 2.0 * spread * cube


def fits(layout):
    n = layout.shape[0]
    tile = NB // n
    place = jnp.arange(NB, dtype=jnp.int32)
    grid = layout.transpose(1, 3, 0, 2)
    rows = jnp.repeat(jnp.repeat(grid[:, 0], tile, 1), tile, 2)
    cols = jnp.repeat(jnp.repeat(grid[:, 1], tile, 1), tile, 2)
    here = (rows == (place % tile)[None, :, None]) & (cols == (place % tile)[None, None, :])
    pattern = jnp.any(here, 0).astype(jnp.float32)
    spread_out = (place[:, None] // tile == jnp.arange(n)[None, :]).astype(jnp.float32)

    def per_tile(side):
        mask = (side == 1).astype(jnp.float32)
        links = pattern * jnp.dot(pattern * mask[None, :], pattern)
        return jnp.dot(spread_out.T, jnp.dot(links, spread_out))

    tiles = place // tile
    right_one = per_tile(tiles % 2)
    left_one = per_tile(tiles // 8)
    total = per_tile(jnp.ones_like(place))
    index = jnp.arange(n, dtype=jnp.int32)
    right_far = jnp.where((index % 2 == 1)[:, None], total - right_one, right_one)
    left_far = jnp.where((index // 8 == 1)[None, :], total - left_one, left_one)
    worst = jnp.maximum(jnp.max(right_far), jnp.max(left_far))
    return (worst <= PACK) & (jnp.max(total) <= TRIPLES)


def plan_of(layout, this_row, this_col):
    n = layout.shape[0]
    tile = NB // n
    k = jnp.arange(n, dtype=jnp.int32)

    def links(row, col):
        left = lax.dynamic_index_in_dim(layout, row, 0, False).transpose(1, 0, 2)
        right = lax.dynamic_index_in_dim(layout, col, 2, False)
        target = lax.dynamic_index_in_dim(left, col, 0, False)
        hit = (left[:, :, None, None, 0] == target[None, None, None, :, 0])
        hit &= left[:, :, None, None, 1] == right[:, None, :, None, 0]
        hit &= right[:, None, :, None, 1] == target[None, None, None, :, 1]
        return hit, left, target

    def order(need):
        flat = need.reshape(-1).astype(jnp.int32)
        return (jnp.cumsum(flat) - flat).reshape(need.shape)

    def picks(need, code, count):
        rank = order(need)
        slot = jnp.arange(count, dtype=jnp.int32)
        chosen = need[None] & (rank[None] == slot[:, None, None])
        return jnp.sum(jnp.where(chosen, code[None], 0), (1, 2))

    hit, left, target = links(this_row, this_col)
    near_right = (k % 2 == this_row % 2)[:, None]
    near_left = (k // 8 == this_col // 8)[:, None]
    slot = jnp.arange(SLOTS, dtype=jnp.int32)[None]
    right_place = (k // 2)[:, None] * SLOTS + slot
    left_place = (k % 8)[:, None] * SLOTS + slot

    other_right = jnp.any(links(this_row + 1 - 2 * (this_row % 2), this_col)[0], (1, 3))
    other_left = jnp.any(links(this_row, (this_col + 8) % n)[0], (2, 3))
    pack_right = picks(other_right & near_right, right_place, PACK)
    pack_left = picks(other_left & near_left, left_place, PACK)

    far_right = jnp.any(hit, (1, 3)) & ~near_right
    far_left = jnp.any(hit, (2, 3)) & ~near_left
    at_right = jnp.where(near_right, right_place, HALF + order(far_right))
    at_left = jnp.where(near_left, left_place, HALF + order(far_left))

    rank = order(hit)
    turn = jnp.arange(TRIPLES, dtype=jnp.int32)
    chosen = hit[None] & (rank[None] == turn[:, None, None, None, None])

    def of_turn(code):
        return jnp.sum(jnp.where(chosen, code[None], 0), (1, 2, 3, 4))

    s_index = jnp.arange(SLOTS, dtype=jnp.int32)
    target_at = of_turn(s_index[None, None, None, :])
    left_at = of_turn(at_left[:, :, None, None])
    right_at = of_turn(at_right[:, None, :, None])
    middle = of_turn((k[:, None] * tile + left[:, :, 1])[:, :, None, None])
    weight = jnp.any(chosen, (1, 2, 3)).astype(jnp.float32)
    whole = jnp.concatenate([target_at, left_at, right_at, pack_right, pack_left])
    part = jnp.concatenate(
        [
            middle.astype(jnp.float32),
            (this_row * tile + target[:, 0]).astype(jnp.float32),
            (this_col * tile + target[:, 1]).astype(jnp.float32),
            weight.reshape(-1),
        ]
    )
    return whole, part


AT_LEFT = TRIPLES
AT_RIGHT = 2 * TRIPLES
AT_PACK_RIGHT = 3 * TRIPLES
AT_PACK_LEFT = 3 * TRIPLES + PACK
AT_ROW = TRIPLES
AT_COL = TRIPLES + SLOTS
AT_WEIGHT = TRIPLES + 2 * SLOTS
AT_SPREAD = AT_WEIGHT + TRIPLES * SLOTS
LINES = AT_SPREAD + 2


def remote(src, dst, sent, came, row, col):
    return pltpu.make_async_remote_copy(
        src_ref=src,
        dst_ref=dst,
        send_sem=sent,
        recv_sem=came,
        device_id=(row, col),
        device_id_type=MESH,
    )


def kernel(
    whole,
    part,
    core_ref,
    band_ref,
    out_ref,
    bands,
    right_pool,
    left_pool,
    square_pool,
    right_out,
    right_in,
    left_out,
    left_in,
    square_out,
    square_in,
    fock,
    square,
    row_vec,
    col_vec,
    mid_vec,
    left_used,
    right_used,
    z_sent,
    z_came,
    x_sent,
    x_came,
    c_sent,
    c_came,
    y_sent,
    y_came,
    b_sent,
    b_came,
):
    row = lax.axis_index("row")
    col = lax.axis_index("col")
    z, y_lo = row // 2, row % 2
    x, core = col // 2 % NX, col % 2
    z_rows = ((row + 2) % 16, (row + 14) % 16)
    y_row = row + 1 - 2 * y_lo
    base = col - x * 2
    x_cols = (base + (x + 1) % NX * 2, base + (x + NX - 1) % NX * 2)
    core_col = col + 1 - 2 * core
    far_col = (col + 8) % 16

    gate = pltpu.get_barrier_semaphore()
    greet = [(z_rows[0], col), (z_rows[1], col), (y_row, col)]
    greet += [(row, (col + step) % 16) for step in range(1, 16)]
    for partner in greet:
        pl.semaphore_signal(gate, inc=1, device_id=partner, device_id_type=MESH)
    pl.semaphore_wait(gate, len(greet))

    started = []

    def send(copy):
        copy.start()
        started.append(copy)

    def z_tile(way, distance):
        return (z + (NZ - distance if way == 0 else distance)) % NZ

    def z_copy(way, d, b, incoming):
        tile = z_tile(way, d if incoming else d - 1)
        place = right_pool.at[tile * SLOTS + b]
        src = core_ref.at[b] if d == 1 and not incoming else place
        sems = z_sent.at[way, d - 1, b], z_came.at[way, d - 1, b]
        return remote(src, place, *sems, z_rows[way], col)

    def z_has(way, d, b):
        return d < 4 or (d == 4 and b // 2 == way)

    def z_take(d, b):
        for way in range(2):
            if z_has(way, d, b):
                z_copy(way, d, b, True).wait_recv()
                if z_has(way, d + 1, b):
                    send(z_copy(way, d + 1, b, False))

    def x_tile(way, distance):
        return (x + (NX - distance if way == 0 else distance)) % NX * 2 + core

    def x_copy(own, pool, turn, way, d, b, incoming):
        tile = x_tile(way, d if incoming else d - 1)
        place = pool.at[tile * SLOTS + b]
        src = own.at[b] if d == 1 and not incoming else place
        sems = x_sent.at[turn, way, d - 1, b], x_came.at[turn, way, d - 1, b]
        return remote(src, place, *sems, row, x_cols[way])

    def x_has(way, d, b):
        return d < 2 or (d == 2 and b // 2 == way)

    def x_take(own, pool, turn, d, b):
        for way in range(2):
            if x_has(way, d, b):
                x_copy(own, pool, turn, way, d, b, True).wait_recv()
                if x_has(way, d + 1, b):
                    send(x_copy(own, pool, turn, way, d + 1, b, False))

    def c_copy(own, pool, turn, at, incoming):
        tile = (x + at) % NX * 2
        tile = tile + (1 - core if incoming else core)
        place = pool.at[pl.ds(tile * SLOTS, SLOTS)]
        src = own if at == 0 and not incoming else place
        return remote(src, place, c_sent.at[turn, at], c_came.at[turn, at], row, core_col)

    def x_start(own, pool, turn):
        for b in range(SLOTS):
            for way in range(2):
                send(x_copy(own, pool, turn, way, 1, b, False))
        send(c_copy(own, pool, turn, 0, False))

    def pack(pool, staging, first):
        for j in range(PACK):
            staging[j] = pool[whole[first + j]]

    def y_copy(staging, landing, turn, there):
        return remote(staging, landing, y_sent.at[turn], y_came.at[turn], *there)

    def band_copy(step, incoming):
        owner = (col + 16 - step) % 16 if incoming else col
        place = bands.at[owner]
        src = place if incoming else band_ref
        sems = b_sent.at[step - 1], b_came.at[step - 1]
        return remote(src, place, *sems, row, (col + step) % 16)

    for b in range(SLOTS):
        for way in range(2):
            send(z_copy(way, 1, b, False))
    for step in range(1, 16):
        send(band_copy(step, False))
    x_start(core_ref, left_pool, 0)

    bands[col] = band_ref[...]
    right_pool[pl.ds(z * SLOTS, SLOTS)] = core_ref[...]
    left_pool[pl.ds((x * 2 + core) * SLOTS, SLOTS)] = core_ref[...]

    for b in range(SLOTS):
        z_take(1, b)
        x_take(core_ref, left_pool, 0, 1, b)
    send(c_copy(core_ref, left_pool, 0, 1, False))
    send(c_copy(core_ref, left_pool, 0, 3, False))

    for step in range(1, 16):
        band_copy(step, True).wait_recv()

    def vectors_on(block):
        return jnp.sum(jnp.where(bands[:, 1] == block, bands[:, 0], 0.0), axis=1)

    def outer(left, right):
        return lax.dot_general(
            left,
            right,
            (((0,), (0,)), ((), ())),
            precision=highest,
            preferred_element_type=jnp.float32,
        )

    for s in range(SLOTS):
        row_vec[s] = vectors_on(part[AT_ROW + s])
        col_vec[s] = vectors_on(part[AT_COL + s])

    z_take(2, 0)
    z_take(2, 1)
    for t in range(TRIPLES):
        mid_vec[t] = vectors_on(part[t])
    z_take(2, 2)
    z_take(2, 3)

    for b in range(SLOTS):
        x_take(core_ref, left_pool, 0, 2, b)
    send(c_copy(core_ref, left_pool, 0, 2, False))
    for at in range(NX):
        c_copy(core_ref, left_pool, 0, at, True).wait_recv()
    pack(left_pool, left_out, AT_PACK_LEFT)
    send(y_copy(left_out, left_in, 0, (row, far_col)))

    for s in range(SLOTS):
        fock[s] = core_ref[s] - outer(row_vec[s], col_vec[s])

    for b in range(SLOTS):
        z_take(3, b)

    def pooled(pool, landing, at):
        near = pool[jnp.minimum(at, HALF - 1)]
        far = landing[jnp.maximum(at - HALF, 0)]
        return jnp.where(at < HALF, near, far)

    inverse = part[AT_SPREAD + 1]
    y_copy(left_out, left_in, 0, (row, far_col)).wait_recv()
    for t in range(TRIPLES):
        block = pooled(left_pool, left_in, whole[AT_LEFT + t])
        left_used[t] = (block - outer(row_vec[whole[t]], mid_vec[t])) * inverse

    for b in range(SLOTS):
        z_take(4, b)
    pack(right_pool, right_out, AT_PACK_RIGHT)
    send(y_copy(right_out, right_in, 1, (y_row, col)))
    y_copy(right_out, right_in, 1, (y_row, col)).wait_recv()

    def product(left, right):
        return jnp.dot(left, right, precision=highest, preferred_element_type=jnp.float32)

    def weighted(target, blocks):
        total = blocks[0] * part[AT_WEIGHT + target]
        for t in range(1, TRIPLES):
            total = total + blocks[t] * part[AT_WEIGHT + t * SLOTS + target]
        return total

    for t in range(TRIPLES):
        block = pooled(right_pool, right_in, whole[AT_RIGHT + t])
        right_used[t] = (block - outer(mid_vec[t], col_vec[whole[t]])) * inverse
        left_used[t] = product(left_used[t], right_used[t])
    for s in range(SLOTS):
        square[s] = weighted(s, left_used)

    x_start(square, square_pool, 1)
    square_pool[pl.ds((x * 2 + core) * SLOTS, SLOTS)] = square[...]
    for b in range(SLOTS):
        x_take(square, square_pool, 1, 1, b)
    send(c_copy(square, square_pool, 1, 1, False))
    send(c_copy(square, square_pool, 1, 3, False))
    for b in range(SLOTS):
        x_take(square, square_pool, 1, 2, b)
    send(c_copy(square, square_pool, 1, 2, False))
    for at in range(NX):
        c_copy(square, square_pool, 1, at, True).wait_recv()
    pack(square_pool, square_out, AT_PACK_LEFT)
    send(y_copy(square_out, square_in, 2, (row, far_col)))
    y_copy(square_out, square_in, 2, (row, far_col)).wait_recv()

    for t in range(TRIPLES):
        block = pooled(square_pool, square_in, whole[AT_LEFT + t])
        left_used[t] = product(block, right_used[t])
    for s in range(SLOTS):
        cube = weighted(s, left_used)
        out_ref[s] = 1.5 * fock[s] - (2.0 * part[AT_SPREAD]) * cube

    for copy in started:
        copy.wait_send()


def sparse(core_blocks, whole, part, band_vectors, band_blocks):
    blocks = band_blocks.astype(jnp.float32)[:, :, None]
    message = jnp.stack([band_vectors[0], jnp.broadcast_to(blocks[0], band_vectors.shape[1:])])
    support = band_vectors.shape[1]
    f32 = jnp.float32
    block = (BS, BS)
    smem = pl.BlockSpec(memory_space=pltpu.SMEM)
    vmem = pl.BlockSpec(memory_space=pltpu.VMEM)
    dma = pltpu.SemaphoreType.DMA
    return pl.pallas_call(
        kernel,
        out_shape=jax.ShapeDtypeStruct(core_blocks.shape, f32),
        in_specs=[smem, smem, vmem, vmem],
        out_specs=vmem,
        scratch_shapes=[
            pltpu.VMEM((16, 2, support, BS), f32),
            pltpu.VMEM((HALF, *block), f32),
            pltpu.VMEM((HALF, *block), f32),
            pltpu.VMEM((HALF, *block), f32),
            pltpu.VMEM((PACK, *block), f32),
            pltpu.VMEM((PACK, *block), f32),
            pltpu.VMEM((PACK, *block), f32),
            pltpu.VMEM((PACK, *block), f32),
            pltpu.VMEM((PACK, *block), f32),
            pltpu.VMEM((PACK, *block), f32),
            pltpu.VMEM((SLOTS, *block), f32),
            pltpu.VMEM((SLOTS, *block), f32),
            pltpu.VMEM((SLOTS, 16, BS), f32),
            pltpu.VMEM((SLOTS, 16, BS), f32),
            pltpu.VMEM((TRIPLES, 16, BS), f32),
            pltpu.VMEM((TRIPLES, *block), f32),
            pltpu.VMEM((TRIPLES, *block), f32),
            dma((2, 4, SLOTS)),
            dma((2, 4, SLOTS)),
            dma((2, 2, 2, SLOTS)),
            dma((2, 2, 2, SLOTS)),
            dma((2, NX)),
            dma((2, NX)),
            dma((3,)),
            dma((3,)),
            dma((15,)),
            dma((15,)),
        ],
        compiler_params=pltpu.CompilerParams(collective_id=0, has_side_effects=True),
        name="sparse",
    )(whole, part, core_blocks, message)


def on_device(core_blocks, block_coords, band_vectors, band_blocks, spread):
    row_count = lax.axis_size("row")
    column_count = lax.axis_size("col")
    layout = block_coords.reshape(row_count, SLOTS, column_count, 2)
    whole, part = plan_of(layout, lax.axis_index("row"), lax.axis_index("col"))
    part = jnp.concatenate([part, jnp.stack([spread, 1.0 / spread])])
    return lax.cond(
        fits(layout),
        lambda: sparse(core_blocks, whole, part, band_vectors, band_blocks),
        lambda: general(core_blocks, block_coords, band_vectors, band_blocks, spread),
    )


def solution(mesh):
    placed = (P("row", "col", None), P(), P("col", None, None), P("col", None), P())
    return jax.shard_map(
        on_device, mesh=mesh, in_specs=placed, out_specs=P("row", "col", None), check_vma=False
    )
```

time: 541 us -> 125 us (0.23)
  starting transfers between devices: 337 us -> 0 us
  Pallas kernels: 0 us -> 104 us
  matrix products: 89.2 us -> 3.63 us
  waiting for transfers between devices: 49.4 us -> 0 us
  blocking collectives: 45.2 us -> 0 us
    ppermute x76 -> x0, starting transfers between devices: 337 us -> none  [shifted(): return lax.ppermute(block, axis, route)]
    pallas_call x0 -> x1, Pallas kernels: none -> 104 us  [sparse(): pl.pallas_call(kernel, out_shape=jax.ShapeDtypeStruct(core_blocks.shape,...]
    dot_general x67 -> x6, matrix products: 89.2 us -> 3.63 us  [per_tile(): return jnp.dot(spread_out.T, jnp.dot(links, spread_out))]
    ppermute x76 -> x0, waiting for transfers between devices: 49.4 us -> none  [shifted(): return lax.ppermute(block, axis, route)]
    all_gather x2 -> x0, blocking collectives: 45.2 us -> none  [the longest x1 26 us: on_device(): lax.all_gather(band_vectors, 'col', axis=0, tiled=True)]
  transfers between devices with their start and end apart: 76 -> 0, of which waited for: 41 -> 0; matrix products, arithmetic and copies ran while one was open for 18% -> 0% of each run, Pallas kernels for 0% -> 0%
where the time goes in v1:
time: 125 us
  Pallas kernels  104 us (83%)
  local copies, waits for them, and re-layouts  8.11 us (6%)
  other arithmetic  6.28 us (5%)
  matrix products  3.63 us (3%)
  between operations  2.94 us (2%)
    pallas_call x1, Pallas kernels, sparse(): pl.pallas_call(kernel, out_shape=jax.ShapeDtypeStruct(core_blocks.shape,...  104 us
    dot_general x6, matrix products, per_tile(): return jnp.dot(spread_out.T, jnp.dot(links, spread_out))  3.63 us

profile of v1, /device:TPU:1, one launch (start us, length us, event | category | flops | bytes accessed | tf_op | source)
XLA Modules:
  0.0 124.7 jit_solution(17666777124536933316)
XLA Ops:
  0.0 0.7 copy-done.1
  0.7 0.2 reshape.1277
  1.0 0.1 copy.204
  1.1 0.1 copy.224
  1.3 0.1 copy.205
  1.4 0.1 copy.216
  1.5 0.1 copy.207
  1.7 0.1 copy.209
  1.8 0.1 copy.206
  2.0 0.1 copy.208
  2.0 0.1 copy.225
  2.1 0.1 broadcast_compare_fusion.4
  2.2 1.7 %fusion.93 = (pred[16,4]{1,0:T(8,128)(4,1)S(1)}, pred[16,4]{1,0:T(8,128)(4,1)S(1)}, pred[16,4,4,4]{3,2,1,0:T(4,128)(4,1)S(1)}) fusion(pred[16,4,4]{2,1,0:T(4,128)(4,1)S(1)} %copy.209, pred[16,4,4]{2,1,0:T(4,128)(4,1)S(1)} %get-tuple-element.792, pred[16,4,4]{2,1,0:T(4,128)(4,1)S(1)} %copy.205), kind=kLoop, calls=%fused_computation.224 | loop fusion | flops 3968 | bytes 1920 | tf_op jit(solution)/shard_map/reduce_or | solution.py:185
  3.9 0.2 reshape.1287
  4.1 0.3 reduce-window.21
  4.4 0.2 reshape.1280
  4.7 0.1 slice_reduce_fusion
  4.9 0.1 add_subtract_fusion
  5.0 0.2 copy.211
  5.2 0.2 copy.210
  5.4 0.4 fusion.42
  5.8 0.1 copy.232
  5.9 0.1 reshape.1292
  6.2 0.1 reduce-window.25
  6.3 0.1 reduce.2
  6.6 0.1 copy.213
  6.8 0.1 reduce-window.26
  6.9 0.1 reduce.3
  7.1 0.1 iota_add_fusion
  7.2 0.1 copy.215
  7.3 0.5 select_reduce_fusion
  8.5 0.1 concatenate.7
  8.6 0.1 copy.226
  8.7 0.1 copy.227
  9.0 0.1 reduce-window.36
  9.1 0.1 reduce.5
  9.4 0.1 copy.228
  9.6 0.3 select_reduce_fusion.4
  9.9 0.1 copy.218
  10.0 0.1 copy.219
  10.3 0.1 reduce-window.29
  10.4 0.1 reduce.4
  10.7 0.1 copy.220
  10.9 0.3 select_reduce_fusion.5
  11.3 0.2 copy.196
  11.5 0.2 broadcast_in_dim.132
  11.7 0.3 reshape.1278
  12.0 0.2 copy.197
  12.1 0.2 broadcast_in_dim.134
  12.3 0.3 reshape.1279
  12.6 0.2 and_reduce_fusion
  12.9 0.1 copy.199
  13.0 0.1 broadcast_select_fusion.12
  13.2 0.3 fusion.39
  13.6 0.3 fusion.40
  13.9 0.9 fusion.96
  14.8 0.8 fusion.65
  15.7 0.3 fusion.38
  16.0 0.9 fusion.70
  18.9 0.6 copy-done.3
  19.6 104.4 %conditional.1 = (f32[4,128,128]{2,1,0:T(8,128)S(1)}) conditional(s32[]{:T(128)} %convert_element_type.139, (s32[1,16]{1,0:T(1,128)S(1)}, s32[64,32]{0,1:T(8,128)S(1)}, f32[1,16,128]{2,1,0:T(8,128)S(1)}, f32[4,128,128]{2,1,0:T(8,128)S(1)}, f32[]{:T(128)}) %tuple.175, (s32[1,16]{1,0:T(1,128)S(1)}, f32[1,16,128]{2,1,0:T(8,128)S(1)}, ...), branch_computations={%region_21.26_spmd, %region_26.27_spmd} | conditional | flops 847645184 | bytes 37009576 | solution.py:532
  19.6 0.6 pad_maximum_fusion.band_ref
  20.3 103.7 %sparse.1 = f32[4,128,128]{2,1,0:T(8,128)S(1)} custom-call(s32[84]{0:T(128)S(1)} %get-tuple-element.552.whole, f32[110]{0:T(128)S(1)} %get-tuple-element.553.part, f32[4,128,128]{2,1,0:T(8,128)S(1)} %get-tuple-element.554.core_ref, f32[2,16,128]{2,1,0:T(8,128)} %pad_maximum_fusion.band_ref), custom_call_target="tpu_custom_call" | custom-call | tf_op jit(solution)/shard_map/cond/branch_1_fun/sparse/pallas_call | solution.py:487
  124.0 0.7 copy.291
  (67 shorter events, 2.6 us)
Async XLA Ops:
  0.0 0.7 copy-start.1
  15.7 3.3 %copy-start = (f32[4,128,128]{2,1,0:T(8,128)S(1)}, f32[4,128,128]{2,1,0:T(8,128)}, u32[]{:S(2)}) copy-start(f32[4,128,128]{2,1,0:T(8,128)} %param.11) | copy-start | bytes 786436
  17.0 1.9 %copy-start.2 = (f32[1,16,128]{2,1,0:T(8,128)S(1)}, f32[1,16,128]{2,1,0:T(8,128)}, u32[]{:S(2)}) copy-start(f32[1,16,128]{2,1,0:T(8,128)} %param.13) | copy-start | bytes 24580
  18.9 0.7 copy-start.3

commit v2 on v0

v2 whole, which is shorter than its diff:
```python
import functools

import jax
import jax.numpy as jnp
from jax import lax
from jax.experimental import pallas as pl
from jax.experimental.pallas import tpu as pltpu
from jax.sharding import PartitionSpec as P

NB = 160
BS = 128
SLOTS = 4
MESH = pl.DeviceIdType.MESH

NZ = 8
NX = 4
TILE = 10
ROOM = 20
PAD = 256

highest = lax.Precision.HIGHEST


def shifted(block, axis, distance):
    devices = range(lax.axis_size(axis))
    route = [((i - distance) % len(devices), i) for i in devices]
    return lax.ppermute(block, axis, route)


def exchange_term(vectors, blocks, block_rows, block_cols):
    hit_row = (blocks[:, :, None] == block_rows[None, None, :]).astype(jnp.float32)
    hit_col = (blocks[:, :, None] == block_cols[None, None, :]).astype(jnp.float32)
    vec_row = jnp.einsum("bln,blx->bnx", hit_row, vectors, precision=highest)
    vec_col = jnp.einsum("bln,blx->bnx", hit_col, vectors, precision=highest)
    return -jnp.einsum("bnx,bny->nxy", vec_row, vec_col, precision=highest)


def tile_layout(layout, tile_row, tile_col):
    slots = layout.shape[1]
    start = (tile_row, jnp.int32(0), tile_col, jnp.int32(0))
    return lax.dynamic_slice(layout, start, (1, slots, 1, 2)).reshape(slots, 2)


def link_weights(targets, left_local, piece, right_local, tile_rows):
    row_target = targets[:, None, None, 0]
    col_target = targets[:, None, None, 1]
    row_left = left_local[None, :, None, 0]
    col_left = left_local[None, :, None, 1]
    row_right = right_local[None, None, :, 0]
    col_right = right_local[None, None, :, 1]
    keep = (row_left == row_target) & (col_left // tile_rows == piece)
    keep = keep & (col_left % tile_rows == row_right) & (col_right == col_target)
    return keep.astype(jnp.float32)


def accumulate(
    total, targets, left_blocks, left_local, piece, right_blocks, right_local, tile_rows
):
    weight = link_weights(targets, left_local, piece, right_local, tile_rows)
    pairs = jnp.einsum("axk,bky->axby", left_blocks, right_blocks, precision=highest)
    return total + jnp.einsum("tab,axby->txy", weight, pairs, precision=highest)


def align(block, axis, amount):
    for place in range((lax.axis_size(axis) - 1).bit_length()):
        moved = shifted(block, axis, -(1 << place))
        block = jnp.where(amount >> place & 1 == 1, moved, block)
    return block


def shifted_product(left, right, layout, targets, this_row, this_col, tile_rows):
    row_count = lax.axis_size("row")
    left = align(left, "col", this_row)

    def step_body(step, carry):
        total, left, right = carry
        source = (this_row + this_col + step) % row_count
        left_local = tile_layout(layout, this_row, source)
        right_local = tile_layout(layout, source, this_col)
        total = accumulate(
            total, targets, left, left_local, 0, right, right_local, tile_rows
        )
        left = shifted(left, "col", -1)
        right = shifted(right, "row", -1)
        return (total, left, right)

    total, left, right = lax.fori_loop(
        0, row_count, step_body, (jnp.zeros_like(left), left, right)
    )
    return (total, right)


def general(core_blocks, block_coords, band_vectors, band_blocks, spread):
    row_count = lax.axis_size("row")
    column_count = lax.axis_size("col")
    tile_rows = NB // row_count
    tile_columns = NB // column_count
    slots = core_blocks.shape[0]
    this_row = lax.axis_index("row")
    this_col = lax.axis_index("col")
    layout = block_coords.reshape(row_count, slots, column_count, 2)
    targets = tile_layout(layout, this_row, this_col)
    vectors, blocks = (
        lax.all_gather(band_vectors, "col", axis=0, tiled=True),
        lax.all_gather(band_blocks, "col", axis=0, tiled=True),
    )
    block_rows = this_row * tile_rows + targets[:, 0]
    block_cols = this_col * tile_columns + targets[:, 1]
    exchange = exchange_term(vectors, blocks, block_rows, block_cols)
    fock = core_blocks + exchange
    scaled = fock / spread
    right = align(scaled, "row", this_col)
    square, right = shifted_product(
        scaled, right, layout, targets, this_row, this_col, tile_rows
    )
    cube, right = shifted_product(
        square, right, layout, targets, this_row, this_col, tile_rows
    )
    return 1.5 * fock - 2.0 * spread * cube


def iota(shape, axis):
    return lax.broadcasted_iota(jnp.int32, shape, axis)


def ones_where(mask):
    return jnp.where(mask, 1.0, 0.0).astype(jnp.float32)


def times(left, right, precision=None):
    return jnp.dot(left, right, precision=precision, preferred_element_type=jnp.float32)


def outer(left, right):
    return lax.dot_general(
        left,
        right,
        (((0,), (0,)), ((), ())),
        precision=highest,
        preferred_element_type=jnp.float32,
    )


def most_products(coords):
    i, c = iota((PAD, 16), 0), iota((PAD, 16), 1)
    down = (i >= c * TILE) & (i < c * TILE + TILE)
    row_at = jnp.sum(jnp.where(down, i - c * TILE + 1, 0), axis=1, keepdims=True) - 1
    r, j = iota((16, PAD), 0), iota((16, PAD), 1)
    along = (j >= r * TILE) & (j < r * TILE + TILE)
    col_at = jnp.sum(jnp.where(along, j - r * TILE + 1, 0), axis=0, keepdims=True) - 1
    row_at, col_at = row_at.astype(jnp.float32), col_at.astype(jnp.float32)
    down, along = ones_where(down), ones_where(along)
    line, tile = iota((32, 16), 0), iota((32, 16), 1)
    rows = times(coords, ones_where(line == 2 * tile))
    cols = times(coords, ones_where(line == 2 * tile + 1))
    pattern = jnp.zeros((PAD, PAD), jnp.float32)
    for s in range(SLOTS):
        of_slot = ones_where(iota((16, 64), 1) == iota((16, 64), 0) * SLOTS + s)
        q = times(times(down, times(of_slot, rows)), along)
        p = times(times(down, times(of_slot, cols)), along)
        pattern = jnp.where((q == row_at) & (p == col_at), 1.0, pattern)
    links = pattern * times(pattern, pattern)
    return jnp.max(times(times(along, links), down))


def products_here(coords, row, col):
    line, lane = iota((64, 32), 0), iota((64, 32), 1)
    high, wide = iota((64, 64), 0), iota((64, 64), 1)
    i, pair = iota((64, 16), 0), iota((64, 16), 1)

    def at_lane(array, place):
        return jnp.sum(jnp.where(lane == place, array, 0.0), axis=1, keepdims=True)

    strip = times(ones_where(wide == row * SLOTS + (high & 3)), coords)
    left_row = at_lane(strip, (line >> 2) * 2)
    left_col = at_lane(strip, (line >> 2) * 2 + 1)
    here_row, here_col = at_lane(coords, col * 2), at_lane(coords, col * 2 + 1)
    same_tile = ones_where((high >> 2) == (wide >> 2))
    of_right = (i & 3) == (pair >> 2)
    right_row = times(same_tile, jnp.where(of_right, here_row, 0.0))
    right_col = times(same_tile, jnp.where(of_right, here_col, 0.0))
    of_target = i == row * SLOTS + (pair & 3)
    everywhere = jnp.ones((64, 64), jnp.float32)
    target_row = times(everywhere, jnp.where(of_target, here_row, 0.0))
    target_col = times(everywhere, jnp.where(of_target, here_col, 0.0))
    hit = (left_row == target_row) & (left_col == right_row) & (right_col == target_col)
    found = ones_where(hit)
    in_line = jnp.broadcast_to(jnp.sum(found, axis=1, keepdims=True), (64, 16))
    before = ones_where(iota((16, 16), 0) < iota((16, 16), 1))
    rank = times(ones_where(wide < high), in_line) + times(found, before)
    rank = jnp.where(hit, rank, -1.0)
    code = (i * 16 + pair).astype(jnp.float32) + 1024.0 * left_col
    number = jnp.sum(found)
    codes = [jnp.sum(jnp.where(rank == float(t), code, 0.0)) for t in range(ROOM)]
    return number, [c.astype(jnp.int32) for c in codes]


def kernel(
    spread,
    coords_ref,
    core_ref,
    vector_ref,
    block_ref,
    out_ref,
    most_ref,
    message,
    bands,
    right_pool,
    left_pool,
    square_pool,
    fock,
    square,
    row_vec,
    col_vec,
    mid_vec,
    left_used,
    right_used,
    sent,
    z_came,
    y_came,
    far_came,
    x_came,
    c_came,
    b_came,
    far2_came,
    x2_came,
    c2_came,
):
    row = lax.axis_index("row")
    col = lax.axis_index("col")
    z, y_lo = row // 2, row % 2
    y_hi, x, core = col // 8, col // 2 % NX, col % 2
    z_rows = ((row + 2) % 16, (row + 14) % 16)
    y_row = row + 1 - 2 * y_lo
    base = col - x * 2
    x_cols = (base + (x + 1) % NX * 2, base + (x + NX - 1) % NX * 2)
    core_col = col + 1 - 2 * core
    far_col = (col + 8) % 16

    gate = pltpu.get_barrier_semaphore()
    greet = [(z_rows[0], col), (z_rows[1], col), (y_row, col)]
    greet += [(row, (col + step) % 16) for step in range(1, 16)]
    for partner in greet:
        pl.semaphore_signal(gate, inc=1, device_id=partner, device_id_type=MESH)

    support = vector_ref.shape[1]
    on_diagonal = iota((support, support), 0) == iota((support, support), 1)
    block_of = jnp.sum(jnp.where(on_diagonal, block_ref[...], 0), axis=1, keepdims=True)
    message[0] = vector_ref[0]
    message[1] = jnp.broadcast_to(block_of.astype(jnp.float32), (support, BS))
    bands[col] = message[...]
    right_pool[pl.ds(row * SLOTS, SLOTS)] = core_ref[...]
    left_pool[pl.ds(col * SLOTS, SLOTS)] = core_ref[...]

    pl.semaphore_wait(gate, len(greet))

    blocks_sent = [0, 0, 0, 0]

    def remote(src, dst, came, to_row, to_col, kind):
        return pltpu.make_async_remote_copy(
            src_ref=src,
            dst_ref=dst,
            send_sem=sent.at[kind],
            recv_sem=came,
            device_id=(to_row, to_col),
            device_id_type=MESH,
        )

    def send(copy, blocks, kind):
        copy.start()
        blocks_sent[kind] += blocks

    OWN_LATE, OWN_EARLY, FAR_EARLY = (2, 0), (0, 0), (0, 1)
    ITEMS = (OWN_LATE, OWN_EARLY, FAR_EARLY)

    def turned(at, size, way, distance):
        return (at + (size - distance if way == 0 else distance)) % size

    def span(first, way, last):
        return (first + way, 1) if last else (first, 2)

    def z_copy(way, d, item, incoming):
        first, far = item
        tile = turned(z, NZ, way, d if incoming else d - 1)
        plane = 1 - y_lo if far else y_lo
        at, size = span(first, way, d == 4)
        place = right_pool.at[pl.ds((tile * 2 + plane) * SLOTS + at, size)]
        own = d == 1 and not far and not incoming
        src = core_ref.at[pl.ds(at, size)] if own else place
        came = z_came.at[way, d - 1, ITEMS.index(item)]
        return remote(src, place, came, z_rows[way], col, 0), size, 0

    def y_copy(way, d, first, incoming):
        tile = z if d == 0 else turned(z, NZ, way, d)
        plane = 1 - y_lo if incoming else y_lo
        at, size = span(first, way, d == 4)
        place = right_pool.at[pl.ds((tile * 2 + plane) * SLOTS + at, size)]
        src = core_ref.at[pl.ds(at, size)] if d == 0 and not incoming else place
        came = y_came.at[way, d] if d else y_came.at[first // 2, 0]
        return remote(src, place, came, y_row, col, 1), size, 1

    def z_take(d, item):
        for way in range(2):
            z_copy(way, d, item, True)[0].wait_recv()
            if d < 4:
                send(*z_copy(way, d + 1, item, False))
            if item == OWN_LATE:
                send(*y_copy(way, d, 2, False))

    def left_tile(way, d, far):
        return ((1 - y_hi if far else y_hi) * 8) + turned(x, NX, way, d) * 2

    def c_send(own, pool, came, way, d, far, at, size):
        kind = 2 if pool is left_pool else 3
        place = pool.at[pl.ds((left_tile(way, d, far) + core) * SLOTS + at, size)]
        src = own.at[pl.ds(at, size)] if d == 0 and not far else place
        send(remote(src, place, came.at[0], row, core_col, kind), size, kind)

    def c_wait(pool, came):
        place = pool.at[pl.ds(0, 32)]
        remote(place, place, came.at[0], row, core_col, 2).wait_recv()

    def far_whole(incoming):
        place = left_pool.at[pl.ds((left_tile(0, 0, incoming) + core) * SLOTS, SLOTS)]
        src = place if incoming else core_ref
        return remote(src, place, far_came.at[0], row, far_col, 1), SLOTS, 1

    def x_whole(way, d, far, incoming):
        tile = left_tile(way, d if incoming else d - 1, far) + core
        at, size = (0, SLOTS) if d == 1 else (2 * way, 2)
        place = left_pool.at[pl.ds(tile * SLOTS + at, size)]
        src = core_ref if d == 1 and not far and not incoming else place
        return remote(src, place, x_came.at[way, d - 1, far], row, x_cols[way], 1), size, 1

    def x_take(d, far):
        for way in range(2):
            x_whole(way, d, far, True)[0].wait_recv()
            if d == 1:
                send(*x_whole(way, 2, far, False))
            at, size = (0, SLOTS) if d == 1 else (2 * way, 2)
            c_send(core_ref, left_pool, c_came, way, d, far, at, size)

    send(*y_copy(0, 0, 0, False))
    for way in range(2):
        send(*z_copy(way, 1, OWN_LATE, False))
    send(*y_copy(0, 0, 2, False))
    for way in range(2):
        send(*z_copy(way, 1, OWN_EARLY, False))

    def band_copy(step):
        return pltpu.make_async_remote_copy(
            src_ref=message,
            dst_ref=bands.at[col],
            send_sem=sent.at[4],
            recv_sem=b_came.at[0],
            device_id=(row, (col + step) % 16),
            device_id_type=MESH,
        )

    for step in range(1, 16):
        band_copy(step).start()
    send(*far_whole(False))
    for way in range(2):
        send(*x_whole(way, 1, 0, False))
    c_send(core_ref, left_pool, c_came, 0, 0, 0, 0, SLOTS)

    coords = coords_ref[...].astype(jnp.float32)
    number, codes = products_here(coords, row, col)

    y_copy(0, 0, 0, True)[0].wait_recv()
    for way in range(2):
        send(*z_copy(way, 1, FAR_EARLY, False))

    most_ref[0] = most_products(coords)

    z_take(1, OWN_LATE)

    at_line, at_lane = iota((64, 32), 0), iota((64, 32), 1)

    def coordinate(s, which):
        mask = (at_line == row * SLOTS + s) & (at_lane == col * 2 + which)
        return jnp.sum(jnp.where(mask, coords, 0.0))

    def vectors_on(block):
        return jnp.sum(jnp.where(bands[:, 1] == block, bands[:, 0], 0.0), axis=1)

    many = bands.at[pl.ds(0, 15)]
    all_bands = pltpu.make_async_remote_copy(
        src_ref=many,
        dst_ref=many,
        send_sem=sent.at[4],
        recv_sem=b_came.at[0],
        device_id=(row, core_col),
        device_id_type=MESH,
    )
    all_bands.wait_recv()
    row_base, col_base = (row * TILE).astype(jnp.float32), (col * TILE).astype(jnp.float32)
    for s in range(SLOTS):
        row_vec[s] = vectors_on(row_base + coordinate(s, 0))
        col_vec[s] = vectors_on(col_base + coordinate(s, 1))

    left_at = [(c >> 4) & 63 for c in codes]
    right_at = [((c >> 6) & 15) * SLOTS + ((c >> 2) & 3) for c in codes]
    target_at = [c & 3 for c in codes]
    middle = [((c >> 6) & 15) * TILE + (c >> 10) for c in codes]

    def middles(first, last):
        for t in range(first, last):
            mid_vec[t] = vectors_on(middle[t].astype(jnp.float32))

    z_take(1, OWN_EARLY)
    x_take(1, 0)
    far_whole(True)[0].wait_recv()
    for way in range(2):
        send(*x_whole(way, 1, 1, False))
    c_send(core_ref, left_pool, c_came, 0, 0, 1, 0, SLOTS)
    middles(0, 5)
    z_take(1, FAR_EARLY)
    middles(5, 10)
    z_take(2, OWN_LATE)
    middles(10, 15)
    x_take(2, 0)
    x_take(1, 1)
    z_take(2, OWN_EARLY)
    middles(15, ROOM)
    z_take(2, FAR_EARLY)

    for s in range(SLOTS):
        fock[s] = core_ref[s] - outer(row_vec[s], col_vec[s])

    def right_terms(first, last):
        for t in range(first, last):
            right_used[t] = outer(mid_vec[t], col_vec[target_at[t]])

    right_terms(0, 10)
    z_take(3, OWN_LATE)
    right_terms(10, ROOM)
    x_take(2, 1)
    c_wait(left_pool, c_came)

    inverse = 1.0 / jnp.full((1, BS), spread[0], jnp.float32)
    scale = inverse * inverse

    def left_terms(first, last):
        for t in range(first, last):
            exchange = outer(row_vec[target_at[t]], mid_vec[t])
            left_used[t] = (left_pool[left_at[t]] - exchange) * scale

    left_terms(0, 6)
    z_take(3, OWN_EARLY)
    left_terms(6, 12)
    z_take(3, FAR_EARLY)
    left_terms(12, 16)
    z_take(4, OWN_LATE)
    left_terms(16, ROOM)
    z_take(4, OWN_EARLY)
    z_take(4, FAR_EARLY)
    y_copy(0, 0, 2, True)[0].wait_recv()
    for d in range(1, 5):
        for way in range(2):
            y_copy(way, d, 2, True)[0].wait_recv()

    def weight(t, s):
        live = (number > float(t)) & (target_at[t] == s)
        return jnp.where(live, 1.0, 0.0).astype(jnp.float32)

    weights = [[weight(t, s) for s in range(SLOTS)] for t in range(ROOM)]

    def weighted(s):
        total = left_used[0] * weights[0][s]
        for t in range(1, ROOM):
            total = total + left_used[t] * weights[t][s]
        return total

    for t in range(ROOM):
        block = right_pool[right_at[t]] - right_used[t]
        right_used[t] = block
        left_used[t] = times(left_used[t], block, highest)
    for s in range(SLOTS):
        square[s] = weighted(s)

    def far_copy(way, d, first, incoming):
        at, size = span(first, way, d == 2)
        tile = left_tile(way, d, incoming) + core
        place = square_pool.at[pl.ds(tile * SLOTS + at, size)]
        src = square.at[pl.ds(at, size)] if d == 0 and not incoming else place
        came = far2_came.at[way, d] if d else far2_came.at[first // 2, 0]
        return remote(src, place, came, row, far_col, 3), size, 3

    def x_copy(way, d, item, incoming):
        first, far = item
        at, size = span(first, way, d == 2)
        tile = left_tile(way, d if incoming else d - 1, far) + core
        place = square_pool.at[pl.ds(tile * SLOTS + at, size)]
        own = d == 1 and not far and not incoming
        src = square.at[pl.ds(at, size)] if own else place
        came = x2_came.at[way, d - 1, ITEMS.index(item)]
        return remote(src, place, came, row, x_cols[way], 3), size, 3

    def x2_take(d, item):
        first, far = item
        for way in range(2):
            x_copy(way, d, item, True)[0].wait_recv()
            if d == 1:
                send(*x_copy(way, 2, item, False))
            if item == OWN_LATE:
                send(*far_copy(way, d, 2, False))
            c_send(square, square_pool, c2_came, way, d, far, *span(first, way, d == 2))

    def far2_take(way, d, first):
        far_copy(way, d, first, True)[0].wait_recv()
        c_send(square, square_pool, c2_came, way, d, 1, *span(first, way, d == 2))

    send(*far_copy(0, 0, 0, False))
    for way in range(2):
        send(*x_copy(way, 1, OWN_LATE, False))
    send(*far_copy(0, 0, 2, False))
    for way in range(2):
        send(*x_copy(way, 1, OWN_EARLY, False))
    c_send(square, square_pool, c2_came, 0, 0, 0, 0, SLOTS)
    square_pool[pl.ds(col * SLOTS, SLOTS)] = square[...]
    x2_take(1, OWN_LATE)
    far2_take(0, 0, 0)
    for way in range(2):
        send(*x_copy(way, 1, FAR_EARLY, False))
    x2_take(1, OWN_EARLY)
    x2_take(2, OWN_LATE)
    far2_take(0, 0, 2)
    x2_take(1, FAR_EARLY)
    x2_take(2, OWN_EARLY)
    far2_take(0, 1, 2)
    far2_take(1, 1, 2)
    x2_take(2, FAR_EARLY)
    far2_take(0, 2, 2)
    far2_take(1, 2, 2)
    c_wait(square_pool, c2_came)

    for t in range(ROOM):
        left_used[t] = times(square_pool[left_at[t]], right_used[t], highest)
    for s in range(SLOTS):
        out_ref[s] = 1.5 * fock[s] - 2.0 * weighted(s)

    all_bands.wait_send()
    for kind, blocks in enumerate(blocks_sent):
        place = right_pool.at[pl.ds(0, blocks)]
        remote(place, place, far_came.at[0], row, core_col, kind).wait_send()


def sparse(core_blocks, block_coords, band_vectors, band_blocks, spread):
    support = band_vectors.shape[1]
    f32 = jnp.float32
    block = (BS, BS)
    smem = pl.BlockSpec(memory_space=pltpu.SMEM)
    vmem = pl.BlockSpec(memory_space=pltpu.VMEM)
    dma = pltpu.SemaphoreType.DMA
    return pl.pallas_call(
        kernel,
        out_shape=(
            jax.ShapeDtypeStruct(core_blocks.shape, f32),
            jax.ShapeDtypeStruct((1,), f32),
        ),
        in_specs=[smem, vmem, vmem, vmem, vmem],
        out_specs=(vmem, smem),
        scratch_shapes=[
            pltpu.VMEM((2, support, BS), f32),
            pltpu.VMEM((16, 2, support, BS), f32),
            pltpu.VMEM((64, *block), f32),
            pltpu.VMEM((64, *block), f32),
            pltpu.VMEM((64, *block), f32),
            pltpu.VMEM((SLOTS, *block), f32),
            pltpu.VMEM((SLOTS, *block), f32),
            pltpu.VMEM((SLOTS, 16, BS), f32),
            pltpu.VMEM((SLOTS, 16, BS), f32),
            pltpu.VMEM((ROOM, 16, BS), f32),
            pltpu.VMEM((ROOM, *block), f32),
            pltpu.VMEM((ROOM, *block), f32),
            dma((5,)),
            dma((2, 4, 3)),
            dma((2, 5)),
            dma((1,)),
            dma((2, 2, 2)),
            dma((1,)),
            dma((1,)),
            dma((2, 3)),
            dma((2, 2, 3)),
            dma((1,)),
        ],
        compiler_params=pltpu.CompilerParams(collective_id=0, has_side_effects=True),
        name="sparse",
    )(spread.reshape(1), block_coords, core_blocks, band_vectors, band_blocks)


def on_device(core_blocks, block_coords, band_vectors, band_blocks, spread):
    arguments = (core_blocks, block_coords, band_vectors, band_blocks, spread)
    purified, most = sparse(*arguments)
    return lax.cond(most[0] <= ROOM, lambda: purified, lambda: general(*arguments))


def solution(mesh):
    placed = (P("row", "col", None), P(), P("col", None, None), P("col", None), P())
    return jax.shard_map(
        on_device, mesh=mesh, in_specs=placed, out_specs=P("row", "col", None), check_vma=False
    )
```

time: 541 us -> 73.4 us (0.14)
  starting transfers between devices: 337 us -> 0 us
  matrix products: 89.2 us -> 0 us
  Pallas kernels: 0 us -> 69 us
  waiting for transfers between devices: 49.4 us -> 0 us
  blocking collectives: 45.2 us -> 0 us
  other arithmetic: 9.19 us -> 0 us
    ppermute x76 -> x0, starting transfers between devices: 337 us -> none  [shifted(): return lax.ppermute(block, axis, route)]
    dot_general x67 -> x0, matrix products: 89.2 us -> none  [the longest x32 57 us: accumulate(): return total + jnp.einsum('tab,axby->txy', weight, pairs, precision=highest)]
    pallas_call x0 -> x1, Pallas kernels: none -> 69 us  [sparse(): pl.pallas_call(kernel, out_shape=(jax.ShapeDtypeStruct(core_blocks.shape,...]
    ppermute x76 -> x0, waiting for transfers between devices: 49.4 us -> none  [shifted(): return lax.ppermute(block, axis, route)]
    all_gather x2 -> x0, blocking collectives: 45.2 us -> none  [the longest x1 26 us: on_device(): lax.all_gather(band_vectors, 'col', axis=0, tiled=True)]
  transfers between devices with their start and end apart: 76 -> 0, of which waited for: 41 -> 0; matrix products, arithmetic and copies ran while one was open for 18% -> 0% of each run, Pallas kernels for 0% -> 0%
where the time goes in v2:
time: 73.4 us; the launch traced here: 73.1 us
  Pallas kernels  69 us (94%)
  local copies, waits for them, and re-layouts  2.8 us (4%)
  between operations  1.32 us (2%)
    pallas_call x1, Pallas kernels, sparse(): pl.pallas_call(kernel, out_shape=(jax.ShapeDtypeStruct(core_blocks.shape,...  69 us
    unnamed x10, local copies, waits for them, and re-layouts  2.8 us

profile of v2, /device:TPU:1, one launch (start us, length us, event | category | flops | bytes accessed | tf_op | source)
XLA Modules:
  0.0 73.1 jit_solution(14817673425238369034)
XLA Ops:
  0.0 0.0 copy-start
  0.0 1.5 %copy.28.coords_ref = s32[64,32]{1,0:T(8,128)} copy(s32[64,32]{0,1:T(8,128)} %param.12) | data formatting | bytes 16384 | tf_op args[1]
  2.1 0.0 copy-start.1
  2.1 69.0 %sparse.1 = (f32[4,128,128]{2,1,0:T(8,128)S(1)}, f32[1]{0:T(128)}) custom-call(f32[1]{0:T(128)} %bitcast.147.spread, s32[64,32]{1,0:T(8,128)} %copy.28.coords_ref, f32[4,128,128]{2,1,0:T(8,128)} %core_ref.1, f32[1,16,128]{2,1,0:T(8,128)} %vector_ref.1, s32[1,16]{1,0:T(1,128)} %block_ref.1), custom_call_target="tpu_custom_call" | custom-call | tf_op jit(solution)/shard_map/sparse/pallas_call | solution.py:556
  71.1 0.0 copy-start.2
  71.8 0.0 copy-start.3
  71.8 0.0 copy-done
  71.8 0.0 copy-done.1
  71.8 0.0 copy-done.2
  71.8 0.6 copy-done.3
  72.4 0.7 copy.81
  (1 shorter events, 0.0 us)
Async XLA Ops:
  0.0 71.8 %copy-start = (f32[4,128,128]{2,1,0:T(8,128)S(1)}, f32[4,128,128]{2,1,0:T(8,128)}, u32[]{:S(2)}) copy-start(f32[4,128,128]{2,1,0:T(8,128)} %core_ref.1) | copy-start | bytes 786436
  2.1 69.7 %copy-start.1 = (s32[64,32]{0,1:T(8,128)S(1)}, s32[64,32]{0,1:T(8,128)}, u32[]{:S(2)}) copy-start(s32[64,32]{0,1:T(8,128)} %param.12) | copy-start | bytes 24580
  71.1 0.7 copy-start.2
  71.8 0.7 copy-start.3

commit v3 on v2

--- a/solution.py
+++ b/solution.py
@@ -131,6 +131,16 @@
     return jnp.dot(left, right, precision=precision, preferred_element_type=jnp.float32)
 
 
+def halves(block):
+    high = block.astype(jnp.bfloat16)
+    return high, (block - high.astype(jnp.float32)).astype(jnp.bfloat16)
+
+
+def product(left_high, left_low, right_high, right_low):
+    total = times(left_high, right_low) + times(left_low, right_high)
+    return total + times(left_high, right_high)
+
+
 def outer(left, right):
     return lax.dot_general(
         left,
@@ -215,6 +225,10 @@
     mid_vec,
     left_used,
     right_used,
+    left_high,
+    left_low,
+    right_high,
+    right_low,
     sent,
     z_came,
     y_came,
@@ -236,10 +250,11 @@
     x_cols = (base + (x + 1) % NX * 2, base + (x + NX - 1) % NX * 2)
     core_col = col + 1 - 2 * core
     far_col = (col + 8) % 16
+    plane = [(row, y_hi * 8 + (col + step) % 8) for step in range(1, 8)]
 
     gate = pltpu.get_barrier_semaphore()
     greet = [(z_rows[0], col), (z_rows[1], col), (y_row, col)]
-    greet += [(row, (col + step) % 16) for step in range(1, 16)]
+    greet += [(row, far_col)] + plane
     for partner in greet:
         pl.semaphore_signal(gate, inc=1, device_id=partner, device_id_type=MESH)
 
@@ -248,9 +263,6 @@
     block_of = jnp.sum(jnp.where(on_diagonal, block_ref[...], 0), axis=1, keepdims=True)
     message[0] = vector_ref[0]
     message[1] = jnp.broadcast_to(block_of.astype(jnp.float32), (support, BS))
-    bands[col] = message[...]
-    right_pool[pl.ds(row * SLOTS, SLOTS)] = core_ref[...]
-    left_pool[pl.ds(col * SLOTS, SLOTS)] = core_ref[...]
 
     pl.semaphore_wait(gate, len(greet))
 
@@ -340,40 +352,46 @@
             at, size = (0, SLOTS) if d == 1 else (2 * way, 2)
             c_send(core_ref, left_pool, c_came, way, d, far, at, size)
 
-    send(*y_copy(0, 0, 0, False))
-    for way in range(2):
-        send(*z_copy(way, 1, OWN_LATE, False))
-    send(*y_copy(0, 0, 2, False))
-    for way in range(2):
-        send(*z_copy(way, 1, OWN_EARLY, False))
-
-    def band_copy(step):
+    def band_copy(owner, to, came):
         return pltpu.make_async_remote_copy(
-            src_ref=message,
-            dst_ref=bands.at[col],
+            src_ref=message if came or owner is col else bands.at[owner],
+            dst_ref=bands.at[owner],
             send_sem=sent.at[4],
-            recv_sem=b_came.at[0],
-            device_id=(row, (col + step) % 16),
+            recv_sem=b_came.at[came],
+            device_id=to,
             device_id_type=MESH,
         )
 
-    for step in range(1, 16):
-        band_copy(step).start()
+    band_copy(col, (row, far_col), 1).start()
+    send(*y_copy(0, 0, 0, False))
+    for way in range(2):
+        send(*z_copy(way, 1, OWN_LATE, False))
+    for way in range(2):
+        send(*x_whole(way, 1, 0, False))
+    for way in range(2):
+        send(*z_copy(way, 1, OWN_EARLY, False))
     send(*far_whole(False))
-    for way in range(2):
-        send(*x_whole(way, 1, 0, False))
+
+    for partner in plane:
+        band_copy(col, partner, 0).start()
+    send(*y_copy(0, 0, 2, False))
     c_send(core_ref, left_pool, c_came, 0, 0, 0, 0, SLOTS)
-
-    coords = coords_ref[...].astype(jnp.float32)
+    bands[col] = message[...]
+    right_pool[pl.ds(row * SLOTS, SLOTS)] = core_ref[...]
+    left_pool[pl.ds(col * SLOTS, SLOTS)] = core_ref[...]
+
+    unit = ones_where(iota((64, 64), 0) == iota((64, 64), 1))
+    coords = lax.dot_general(
+        unit,
+        coords_ref[...].astype(jnp.float32),
+        (((1,), (1,)), ((), ())),
+        preferred_element_type=jnp.float32,
+    )
     number, codes = products_here(coords, row, col)
 
     y_copy(0, 0, 0, True)[0].wait_recv()
     for way in range(2):
         send(*z_copy(way, 1, FAR_EARLY, False))
-
-    most_ref[0] = most_products(coords)
-
-    z_take(1, OWN_LATE)
 
     at_line, at_lane = iota((64, 32), 0), iota((64, 32), 1)
 
@@ -384,20 +402,18 @@
     def vectors_on(block):
         return jnp.sum(jnp.where(bands[:, 1] == block, bands[:, 0], 0.0), axis=1)
 
-    many = bands.at[pl.ds(0, 15)]
-    all_bands = pltpu.make_async_remote_copy(
-        src_ref=many,
-        dst_ref=many,
-        send_sem=sent.at[4],
-        recv_sem=b_came.at[0],
-        device_id=(row, core_col),
-        device_id_type=MESH,
-    )
-    all_bands.wait_recv()
+    def all_bands(count):
+        many = bands.at[pl.ds(0, count)]
+        return pltpu.make_async_remote_copy(
+            src_ref=many,
+            dst_ref=many,
+            send_sem=sent.at[4],
+            recv_sem=b_came.at[0],
+            device_id=(row, core_col),
+            device_id_type=MESH,
+        )
+
     row_base, col_base = (row * TILE).astype(jnp.float32), (col * TILE).astype(jnp.float32)
-    for s in range(SLOTS):
-        row_vec[s] = vectors_on(row_base + coordinate(s, 0))
-        col_vec[s] = vectors_on(col_base + coordinate(s, 1))
 
     left_at = [(c >> 4) & 63 for c in codes]
     right_at = [((c >> 6) & 15) * SLOTS + ((c >> 2) & 3) for c in codes]
@@ -405,67 +421,70 @@
     middle = [((c >> 6) & 15) * TILE + (c >> 10) for c in codes]
 
     def middles(first, last):
-        for t in range(first, last):
+        for t in range(min(first, ROOM), min(last, ROOM)):
             mid_vec[t] = vectors_on(middle[t].astype(jnp.float32))
 
+    def right_terms(first, last):
+        for t in range(min(first, ROOM), min(last, ROOM)):
+            right_used[t] = outer(mid_vec[t], col_vec[target_at[t]])
+
+    inverse = 1.0 / jnp.full((1, BS), spread[0], jnp.float32)
+    scale = inverse * inverse
+
+    def left_terms(first, last):
+        for t in range(min(first, ROOM), min(last, ROOM)):
+            exchange = outer(row_vec[target_at[t]], mid_vec[t])
+            high, low = halves((left_pool[left_at[t]] - exchange) * scale)
+            left_high[t], left_low[t] = high, low
+
+    z_take(1, OWN_LATE)
+    band_copy(far_col, (row, far_col), 1).wait_recv()
+    for partner in plane:
+        band_copy(far_col, partner, 0).start()
     z_take(1, OWN_EARLY)
     x_take(1, 0)
+    z_take(1, FAR_EARLY)
+    x_take(2, 0)
+    z_take(2, OWN_LATE)
+    all_bands(14).wait_recv()
+    for s in range(SLOTS):
+        row_vec[s] = vectors_on(row_base + coordinate(s, 0))
+        col_vec[s] = vectors_on(col_base + coordinate(s, 1))
     far_whole(True)[0].wait_recv()
     for way in range(2):
         send(*x_whole(way, 1, 1, False))
     c_send(core_ref, left_pool, c_came, 0, 0, 1, 0, SLOTS)
-    middles(0, 5)
-    z_take(1, FAR_EARLY)
-    middles(5, 10)
-    z_take(2, OWN_LATE)
-    middles(10, 15)
-    x_take(2, 0)
-    x_take(1, 1)
+    middles(0, 10)
     z_take(2, OWN_EARLY)
-    middles(15, ROOM)
-    z_take(2, FAR_EARLY)
-
+    middles(10, ROOM)
     for s in range(SLOTS):
         fock[s] = core_ref[s] - outer(row_vec[s], col_vec[s])
-
-    def right_terms(first, last):
-        for t in range(first, last):
-            right_used[t] = outer(mid_vec[t], col_vec[target_at[t]])
-
+    z_take(2, FAR_EARLY)
     right_terms(0, 10)
     z_take(3, OWN_LATE)
     right_terms(10, ROOM)
+    x_take(1, 1)
+    z_take(3, OWN_EARLY)
+    most_ref[0] = most_products(coords)
+    def weight(t, s):
+        live = (number > float(t)) & (target_at[t] == s)
+        return jnp.where(live, 1.0, 0.0).astype(jnp.float32)
+
+    weights = [[weight(t, s) for s in range(SLOTS)] for t in range(ROOM)]
+
+    z_take(3, FAR_EARLY)
     x_take(2, 1)
+    z_take(4, OWN_LATE)
     c_wait(left_pool, c_came)
-
-    inverse = 1.0 / jnp.full((1, BS), spread[0], jnp.float32)
-    scale = inverse * inverse
-
-    def left_terms(first, last):
-        for t in range(first, last):
-            exchange = outer(row_vec[target_at[t]], mid_vec[t])
-            left_used[t] = (left_pool[left_at[t]] - exchange) * scale
-
-    left_terms(0, 6)
-    z_take(3, OWN_EARLY)
-    left_terms(6, 12)
-    z_take(3, FAR_EARLY)
-    left_terms(12, 16)
-    z_take(4, OWN_LATE)
-    left_terms(16, ROOM)
+    left_terms(0, 10)
     z_take(4, OWN_EARLY)
+    left_terms(10, ROOM)
     z_take(4, FAR_EARLY)
     y_copy(0, 0, 2, True)[0].wait_recv()
     for d in range(1, 5):
         for way in range(2):
             y_copy(way, d, 2, True)[0].wait_recv()
 
-    def weight(t, s):
-        live = (number > float(t)) & (target_at[t] == s)
-        return jnp.where(live, 1.0, 0.0).astype(jnp.float32)
-
-    weights = [[weight(t, s) for s in range(SLOTS)] for t in range(ROOM)]
-
     def weighted(s):
         total = left_used[0] * weights[0][s]
         for t in range(1, ROOM):
@@ -473,9 +492,9 @@
         return total
 
     for t in range(ROOM):
-        block = right_pool[right_at[t]] - right_used[t]
-        right_used[t] = block
-        left_used[t] = times(left_used[t], block, highest)
+        high, low = halves(right_pool[right_at[t]] - right_used[t])
+        right_high[t], right_low[t] = high, low
+        left_used[t] = product(left_high[t], left_low[t], high, low)
     for s in range(SLOTS):
         square[s] = weighted(s)
 
@@ -536,11 +555,12 @@
     c_wait(square_pool, c2_came)
 
     for t in range(ROOM):
-        left_used[t] = times(square_pool[left_at[t]], right_used[t], highest)
+        high, low = halves(square_pool[left_at[t]])
+        left_used[t] = product(high, low, right_high[t], right_low[t])
     for s in range(SLOTS):
         out_ref[s] = 1.5 * fock[s] - 2.0 * weighted(s)
 
-    all_bands.wait_send()
+    all_bands(15).wait_send()
     for kind, blocks in enumerate(blocks_sent):
         place = right_pool.at[pl.ds(0, blocks)]
         remote(place, place, far_came.at[0], row, core_col, kind).wait_send()
@@ -574,20 +594,26 @@
             pltpu.VMEM((ROOM, 16, BS), f32),
             pltpu.VMEM((ROOM, *block), f32),
             pltpu.VMEM((ROOM, *block), f32),
+            pltpu.VMEM((ROOM, *block), jnp.bfloat16),
+            pltpu.VMEM((ROOM, *block), jnp.bfloat16),
+            pltpu.VMEM((ROOM, *block), jnp.bfloat16),
+            pltpu.VMEM((ROOM, *block), jnp.bfloat16),
             dma((5,)),
             dma((2, 4, 3)),
             dma((2, 5)),
             dma((1,)),
             dma((2, 2, 2)),
             dma((1,)),
-            dma((1,)),
+            dma((2,)),
             dma((2, 3)),
             dma((2, 2, 3)),
             dma((1,)),
         ],
-        compiler_params=pltpu.CompilerParams(collective_id=0, has_side_effects=True),
+        compiler_params=pltpu.CompilerParams(
+            collective_id=0, has_side_effects=True, vmem_limit_bytes=28 << 20
+        ),
         name="sparse",
-    )(spread.reshape(1), block_coords, core_blocks, band_vectors, band_blocks)
+    )(spread.reshape(1), block_coords.T, core_blocks, band_vectors, band_blocks)
 
 
 def on_device(core_blocks, block_coords, band_vectors, band_blocks, spread):

time: 73.4 us -> 66.6 us (0.907)
  Pallas kernels: 69 us -> 63.7 us
  local copies, waits for them, and re-layouts: 2.8 us -> 1.34 us
    pallas_call x1, Pallas kernels: 69 us -> 63.7 us  [sparse(): pl.pallas_call(kernel, out_shape=(jax.ShapeDtypeStruct(core_blocks.shape,...]
    unnamed x10 -> x9, local copies, waits for them, and re-layouts: 2.8 us -> 1.34 us
where the time goes in v3:
time: 66.6 us; the launch traced here: 66.4 us
  Pallas kernels  63.7 us (96%)
  between operations  1.4 us (2%)
  local copies, waits for them, and re-layouts  1.34 us (2%)
    pallas_call x1, Pallas kernels, sparse(): pl.pallas_call(kernel, out_shape=(jax.ShapeDtypeStruct(core_blocks.shape,...  63.7 us
    unnamed x9, local copies, waits for them, and re-layouts  1.34 us

profile of v3, /device:TPU:1, one launch (start us, length us, event | category | flops | bytes accessed | tf_op | source)
XLA Modules:
  0.0 66.4 jit_solution(16184411779129727089)
XLA Ops:
  0.0 0.0 copy-start
  0.7 0.0 copy-start.1
  0.7 63.7 %sparse.1 = (f32[4,128,128]{2,1,0:T(8,128)S(1)}, f32[1]{0:T(128)}) custom-call(f32[1]{0:T(128)} %bitcast.148.spread, s32[32,64]{1,0:T(8,128)} %bitcast.153, f32[4,128,128]{2,1,0:T(8,128)} %core_ref.1, f32[1,16,128]{2,1,0:T(8,128)} %vector_ref.1, s32[1,16]{1,0:T(1,128)} %block_ref.1), custom_call_target="tpu_custom_call" | custom-call | tf_op jit(solution)/shard_map/sparse/pallas_call | solution.py:576
  64.4 0.0 copy-start.2
  65.0 0.0 copy-start.3
  65.1 0.0 copy-done
  65.1 0.0 copy-done.1
  65.1 0.0 copy-done.2
  65.1 0.6 copy-done.3
  65.7 0.7 %copy.78 = f32[4,128,128]{2,1,0:T(8,128)} copy(f32[4,128,128]{2,1,0:T(8,128)S(1)} %get-tuple-element.547) | data formatting | bytes 524288
  (1 shorter events, 0.0 us)
Async XLA Ops:
  0.0 65.1 %copy-start = (f32[4,128,128]{2,1,0:T(8,128)S(1)}, f32[4,128,128]{2,1,0:T(8,128)}, u32[]{:S(2)}) copy-start(f32[4,128,128]{2,1,0:T(8,128)} %core_ref.1) | copy-start | bytes 786436
  0.7 64.4 %copy-start.1 = (s32[64,32]{0,1:T(8,128)S(1)}, s32[64,32]{0,1:T(8,128)}, u32[]{:S(2)}) copy-start(s32[64,32]{0,1:T(8,128)} %param.12) | copy-start | bytes 24580
  64.4 0.7 %copy-start.2 = (f32[1,16,128]{2,1,0:T(8,128)S(1)}, f32[1,16,128]{2,1,0:T(8,128)}, u32[]{:S(2)}) copy-start(f32[1,16,128]{2,1,0:T(8,128)} %vector_ref.1) | copy-start | bytes 24580
  65.0 0.7 copy-start.3

commit v4 on v3

--- a/solution.py
+++ b/solution.py
@@ -17,6 +17,9 @@
 TILE = 10
 ROOM = 20
 PAD = 256
+ROWS = SLOTS * BS
+EARLY = 240
+EARLY_SQUARE = 272
 
 highest = lax.Precision.HIGHEST
 
@@ -206,13 +209,20 @@
 
 
 def kernel(
+    spread_hbm,
+    coords_hbm,
+    core_hbm,
+    vector_hbm,
+    block_hbm,
+    out_ref,
+    fits_ref,
+    kept_ref,
     spread,
     coords_ref,
-    core_ref,
     vector_ref,
     block_ref,
-    out_ref,
-    most_ref,
+    came,
+    fits_here,
     message,
     bands,
     right_pool,
@@ -258,15 +268,22 @@
     for partner in greet:
         pl.semaphore_signal(gate, inc=1, device_id=partner, device_id_type=MESH)
 
-    support = vector_ref.shape[1]
-    on_diagonal = iota((support, support), 0) == iota((support, support), 1)
-    block_of = jnp.sum(jnp.where(on_diagonal, block_ref[...], 0), axis=1, keepdims=True)
-    message[0] = vector_ref[0]
-    message[1] = jnp.broadcast_to(block_of.astype(jnp.float32), (support, BS))
-
+    tile_rows = pl.ds(pl.multiple_of(row * ROWS, ROWS), ROWS)
+    tile_cols = pl.ds(pl.multiple_of(col * ROWS, ROWS), ROWS)
+    local = [
+        pltpu.make_async_copy(vector_hbm, vector_ref, came.at[0]),
+        pltpu.make_async_copy(block_hbm, block_ref, came.at[1]),
+        pltpu.make_async_copy(coords_hbm, coords_ref, came.at[2]),
+        pltpu.make_async_copy(spread_hbm, spread, came.at[3]),
+        pltpu.make_async_copy(core_hbm, right_pool.at[tile_rows], came.at[4]),
+        pltpu.make_async_copy(core_hbm, left_pool.at[tile_cols], came.at[5]),
+        pltpu.make_async_copy(core_hbm, fock, came.at[6]),
+    ]
+    for copy in local:
+        copy.start()
     pl.semaphore_wait(gate, len(greet))
 
-    blocks_sent = [0, 0, 0, 0]
+    rows_sent = [0, 0, 0, 0]
 
     def remote(src, dst, came, to_row, to_col, kind):
         return pltpu.make_async_remote_copy(
@@ -278,37 +295,41 @@
             device_id_type=MESH,
         )
 
-    def send(copy, blocks, kind):
+    def send(copy, rows, kind):
         copy.start()
-        blocks_sent[kind] += blocks
-
-    OWN_LATE, OWN_EARLY, FAR_EARLY = (2, 0), (0, 0), (0, 1)
+        rows_sent[kind] += rows
+
+    OWN_LATE, OWN_EARLY, FAR_EARLY = (1, 0), (0, 0), (0, 1)
     ITEMS = (OWN_LATE, OWN_EARLY, FAR_EARLY)
 
     def turned(at, size, way, distance):
         return (at + (size - distance if way == 0 else distance)) % size
 
-    def span(first, way, last):
-        return (first + way, 1) if last else (first, 2)
+    def span(late, early, way, last):
+        at, size = (early, ROWS - early) if late else (0, early)
+        return (at + way * (size // 2), size // 2) if last else (at, size)
+
+    def rows_of(pool, tile, at, size):
+        return pool.at[pl.ds(pl.multiple_of(tile * ROWS + at, 8), size)]
 
     def z_copy(way, d, item, incoming):
-        first, far = item
+        late, far = item
         tile = turned(z, NZ, way, d if incoming else d - 1)
         plane = 1 - y_lo if far else y_lo
-        at, size = span(first, way, d == 4)
-        place = right_pool.at[pl.ds((tile * 2 + plane) * SLOTS + at, size)]
+        at, size = span(late, EARLY, way, d == 4)
+        place = rows_of(right_pool, tile * 2 + plane, at, size)
         own = d == 1 and not far and not incoming
-        src = core_ref.at[pl.ds(at, size)] if own else place
+        src = core_hbm.at[pl.ds(at, size)] if own else place
         came = z_came.at[way, d - 1, ITEMS.index(item)]
         return remote(src, place, came, z_rows[way], col, 0), size, 0
 
-    def y_copy(way, d, first, incoming):
+    def y_copy(way, d, late, incoming):
         tile = z if d == 0 else turned(z, NZ, way, d)
         plane = 1 - y_lo if incoming else y_lo
-        at, size = span(first, way, d == 4)
-        place = right_pool.at[pl.ds((tile * 2 + plane) * SLOTS + at, size)]
-        src = core_ref.at[pl.ds(at, size)] if d == 0 and not incoming else place
-        came = y_came.at[way, d] if d else y_came.at[first // 2, 0]
+        at, size = span(late, EARLY, way, d == 4)
+        place = rows_of(right_pool, tile * 2 + plane, at, size)
+        src = core_hbm.at[pl.ds(at, size)] if d == 0 and not incoming else place
+        came = y_came.at[way, d] if d else y_came.at[late, 0]
         return remote(src, place, came, y_row, col, 1), size, 1
 
     def z_take(d, item):
@@ -317,31 +338,31 @@
             if d < 4:
                 send(*z_copy(way, d + 1, item, False))
             if item == OWN_LATE:
-                send(*y_copy(way, d, 2, False))
+                send(*y_copy(way, d, 1, False))
 
     def left_tile(way, d, far):
         return ((1 - y_hi if far else y_hi) * 8) + turned(x, NX, way, d) * 2
 
     def c_send(own, pool, came, way, d, far, at, size):
         kind = 2 if pool is left_pool else 3
-        place = pool.at[pl.ds((left_tile(way, d, far) + core) * SLOTS + at, size)]
+        place = rows_of(pool, left_tile(way, d, far) + core, at, size)
         src = own.at[pl.ds(at, size)] if d == 0 and not far else place
         send(remote(src, place, came.at[0], row, core_col, kind), size, kind)
 
     def c_wait(pool, came):
-        place = pool.at[pl.ds(0, 32)]
+        place = pool.at[pl.ds(0, 8 * ROWS)]
         remote(place, place, came.at[0], row, core_col, 2).wait_recv()
 
     def far_whole(incoming):
-        place = left_pool.at[pl.ds((left_tile(0, 0, incoming) + core) * SLOTS, SLOTS)]
-        src = place if incoming else core_ref
-        return remote(src, place, far_came.at[0], row, far_col, 1), SLOTS, 1
+        place = rows_of(left_pool, left_tile(0, 0, incoming) + core, 0, ROWS)
+        src = place if incoming else core_hbm
+        return remote(src, place, far_came.at[0], row, far_col, 1), ROWS, 1
 
     def x_whole(way, d, far, incoming):
         tile = left_tile(way, d if incoming else d - 1, far) + core
-        at, size = (0, SLOTS) if d == 1 else (2 * way, 2)
-        place = left_pool.at[pl.ds(tile * SLOTS + at, size)]
-        src = core_ref if d == 1 and not far and not incoming else place
+        at, size = (0, ROWS) if d == 1 else (way * (ROWS // 2), ROWS // 2)
+        place = rows_of(left_pool, tile, at, size)
+        src = core_hbm if d == 1 and not far and not incoming else place
         return remote(src, place, x_came.at[way, d - 1, far], row, x_cols[way], 1), size, 1
 
     def x_take(d, far):
@@ -349,8 +370,8 @@
             x_whole(way, d, far, True)[0].wait_recv()
             if d == 1:
                 send(*x_whole(way, 2, far, False))
-            at, size = (0, SLOTS) if d == 1 else (2 * way, 2)
-            c_send(core_ref, left_pool, c_came, way, d, far, at, size)
+            at, size = (0, ROWS) if d == 1 else (way * (ROWS // 2), ROWS // 2)
+            c_send(core_hbm, left_pool, c_came, way, d, far, at, size)
 
     def band_copy(owner, to, came):
         return pltpu.make_async_remote_copy(
@@ -362,10 +383,19 @@
             device_id_type=MESH,
         )
 
+    send(*y_copy(0, 0, 0, False))
+    for way in range(2):
+        send(*z_copy(way, 1, OWN_LATE, False))
+    for copy in local[:2]:
+        copy.wait()
+
+    support = vector_ref.shape[1]
+    on_diagonal = iota((support, support), 0) == iota((support, support), 1)
+    block_of = jnp.sum(jnp.where(on_diagonal, block_ref[...], 0), axis=1, keepdims=True)
+    message[0] = vector_ref[0]
+    message[1] = jnp.broadcast_to(block_of.astype(jnp.float32), (support, BS))
+
     band_copy(col, (row, far_col), 1).start()
-    send(*y_copy(0, 0, 0, False))
-    for way in range(2):
-        send(*z_copy(way, 1, OWN_LATE, False))
     for way in range(2):
         send(*x_whole(way, 1, 0, False))
     for way in range(2):
@@ -374,11 +404,12 @@
 
     for partner in plane:
         band_copy(col, partner, 0).start()
-    send(*y_copy(0, 0, 2, False))
-    c_send(core_ref, left_pool, c_came, 0, 0, 0, 0, SLOTS)
+    send(*y_copy(0, 0, 1, False))
+    c_send(core_hbm, left_pool, c_came, 0, 0, 0, 0, ROWS)
     bands[col] = message[...]
-    right_pool[pl.ds(row * SLOTS, SLOTS)] = core_ref[...]
-    left_pool[pl.ds(col * SLOTS, SLOTS)] = core_ref[...]
+    kept_ref[...] = message[...]
+    local[2].wait()
+    local[3].wait()
 
     unit = ones_where(iota((64, 64), 0) == iota((64, 64), 1))
     coords = lax.dot_general(
@@ -415,6 +446,9 @@
 
     row_base, col_base = (row * TILE).astype(jnp.float32), (col * TILE).astype(jnp.float32)
 
+    def block_rows(at):
+        return pl.ds(at * BS, BS)
+
     left_at = [(c >> 4) & 63 for c in codes]
     right_at = [((c >> 6) & 15) * SLOTS + ((c >> 2) & 3) for c in codes]
     target_at = [c & 3 for c in codes]
@@ -434,7 +468,7 @@
     def left_terms(first, last):
         for t in range(min(first, ROOM), min(last, ROOM)):
             exchange = outer(row_vec[target_at[t]], mid_vec[t])
-            high, low = halves((left_pool[left_at[t]] - exchange) * scale)
+            high, low = halves((left_pool[block_rows(left_at[t])] - exchange) * scale)
             left_high[t], left_low[t] = high, low
 
     z_take(1, OWN_LATE)
@@ -453,25 +487,29 @@
     far_whole(True)[0].wait_recv()
     for way in range(2):
         send(*x_whole(way, 1, 1, False))
-    c_send(core_ref, left_pool, c_came, 0, 0, 1, 0, SLOTS)
+    c_send(core_hbm, left_pool, c_came, 0, 0, 1, 0, ROWS)
     middles(0, 10)
     z_take(2, OWN_EARLY)
     middles(10, ROOM)
+    for copy in local[4:]:
+        copy.wait()
     for s in range(SLOTS):
-        fock[s] = core_ref[s] - outer(row_vec[s], col_vec[s])
+        fock[block_rows(s)] -= outer(row_vec[s], col_vec[s])
     z_take(2, FAR_EARLY)
     right_terms(0, 10)
     z_take(3, OWN_LATE)
     right_terms(10, ROOM)
     x_take(1, 1)
     z_take(3, OWN_EARLY)
-    most_ref[0] = most_products(coords)
+    fits_here[0] = jnp.where(most_products(coords) <= ROOM, 1, 0).astype(jnp.int32)
     def weight(t, s):
         live = (number > float(t)) & (target_at[t] == s)
         return jnp.where(live, 1.0, 0.0).astype(jnp.float32)
 
     weights = [[weight(t, s) for s in range(SLOTS)] for t in range(ROOM)]
 
+    flag = pltpu.make_async_copy(fits_here, fits_ref, came.at[7])
+    flag.start()
     z_take(3, FAR_EARLY)
     x_take(2, 1)
     z_take(4, OWN_LATE)
@@ -480,10 +518,10 @@
     z_take(4, OWN_EARLY)
     left_terms(10, ROOM)
     z_take(4, FAR_EARLY)
-    y_copy(0, 0, 2, True)[0].wait_recv()
+    y_copy(0, 0, 1, True)[0].wait_recv()
     for d in range(1, 5):
         for way in range(2):
-            y_copy(way, d, 2, True)[0].wait_recv()
+            y_copy(way, d, 1, True)[0].wait_recv()
 
     def weighted(s):
         total = left_used[0] * weights[0][s]
@@ -492,77 +530,79 @@
         return total
 
     for t in range(ROOM):
-        high, low = halves(right_pool[right_at[t]] - right_used[t])
+        high, low = halves(right_pool[block_rows(right_at[t])] - right_used[t])
         right_high[t], right_low[t] = high, low
         left_used[t] = product(left_high[t], left_low[t], high, low)
     for s in range(SLOTS):
-        square[s] = weighted(s)
-
-    def far_copy(way, d, first, incoming):
-        at, size = span(first, way, d == 2)
+        square[block_rows(s)] = weighted(s)
+
+    def far_copy(way, d, late, incoming):
+        at, size = span(late, EARLY_SQUARE, way, d == 2)
         tile = left_tile(way, d, incoming) + core
-        place = square_pool.at[pl.ds(tile * SLOTS + at, size)]
+        place = rows_of(square_pool, tile, at, size)
         src = square.at[pl.ds(at, size)] if d == 0 and not incoming else place
-        came = far2_came.at[way, d] if d else far2_came.at[first // 2, 0]
+        came = far2_came.at[way, d] if d else far2_came.at[late, 0]
         return remote(src, place, came, row, far_col, 3), size, 3
 
     def x_copy(way, d, item, incoming):
-        first, far = item
-        at, size = span(first, way, d == 2)
+        late, far = item
+        at, size = span(late, EARLY_SQUARE, way, d == 2)
         tile = left_tile(way, d if incoming else d - 1, far) + core
-        place = square_pool.at[pl.ds(tile * SLOTS + at, size)]
+        place = rows_of(square_pool, tile, at, size)
         own = d == 1 and not far and not incoming
         src = square.at[pl.ds(at, size)] if own else place
         came = x2_came.at[way, d - 1, ITEMS.index(item)]
         return remote(src, place, came, row, x_cols[way], 3), size, 3
 
     def x2_take(d, item):
-        first, far = item
+        late, far = item
         for way in range(2):
             x_copy(way, d, item, True)[0].wait_recv()
             if d == 1:
                 send(*x_copy(way, 2, item, False))
             if item == OWN_LATE:
-                send(*far_copy(way, d, 2, False))
-            c_send(square, square_pool, c2_came, way, d, far, *span(first, way, d == 2))
-
-    def far2_take(way, d, first):
-        far_copy(way, d, first, True)[0].wait_recv()
-        c_send(square, square_pool, c2_came, way, d, 1, *span(first, way, d == 2))
+                send(*far_copy(way, d, 1, False))
+            c_send(square, square_pool, c2_came, way, d, far, *span(late, EARLY_SQUARE, way, d == 2))
+
+    def far2_take(way, d, late):
+        far_copy(way, d, late, True)[0].wait_recv()
+        at, size = span(late, EARLY_SQUARE, way, d == 2)
+        c_send(square, square_pool, c2_came, way, d, 1, at, size)
 
     send(*far_copy(0, 0, 0, False))
     for way in range(2):
         send(*x_copy(way, 1, OWN_LATE, False))
-    send(*far_copy(0, 0, 2, False))
+    send(*far_copy(0, 0, 1, False))
     for way in range(2):
         send(*x_copy(way, 1, OWN_EARLY, False))
-    c_send(square, square_pool, c2_came, 0, 0, 0, 0, SLOTS)
-    square_pool[pl.ds(col * SLOTS, SLOTS)] = square[...]
+    c_send(square, square_pool, c2_came, 0, 0, 0, 0, ROWS)
+    square_pool[tile_cols] = square[...]
     x2_take(1, OWN_LATE)
     far2_take(0, 0, 0)
     for way in range(2):
         send(*x_copy(way, 1, FAR_EARLY, False))
     x2_take(1, OWN_EARLY)
     x2_take(2, OWN_LATE)
-    far2_take(0, 0, 2)
+    far2_take(0, 0, 1)
     x2_take(1, FAR_EARLY)
     x2_take(2, OWN_EARLY)
-    far2_take(0, 1, 2)
-    far2_take(1, 1, 2)
+    far2_take(0, 1, 1)
+    far2_take(1, 1, 1)
     x2_take(2, FAR_EARLY)
-    far2_take(0, 2, 2)
-    far2_take(1, 2, 2)
+    far2_take(0, 2, 1)
+    far2_take(1, 2, 1)
     c_wait(square_pool, c2_came)
 
     for t in range(ROOM):
-        high, low = halves(square_pool[left_at[t]])
+        high, low = halves(square_pool[block_rows(left_at[t])])
         left_used[t] = product(high, low, right_high[t], right_low[t])
     for s in range(SLOTS):
-        out_ref[s] = 1.5 * fock[s] - 2.0 * weighted(s)
-
+        out_ref[s] = 1.5 * fock[block_rows(s)] - 2.0 * weighted(s)
+
+    flag.wait()
     all_bands(15).wait_send()
-    for kind, blocks in enumerate(blocks_sent):
-        place = right_pool.at[pl.ds(0, blocks)]
+    for kind, rows in enumerate(rows_sent):
+        place = right_pool.at[pl.ds(0, rows)]
         remote(place, place, far_came.at[0], row, core_col, kind).wait_send()
 
 
@@ -571,24 +611,32 @@
     f32 = jnp.float32
     block = (BS, BS)
     smem = pl.BlockSpec(memory_space=pltpu.SMEM)
+    hbm = pl.BlockSpec(memory_space=pltpu.HBM)
     vmem = pl.BlockSpec(memory_space=pltpu.VMEM)
     dma = pltpu.SemaphoreType.DMA
     return pl.pallas_call(
         kernel,
         out_shape=(
             jax.ShapeDtypeStruct(core_blocks.shape, f32),
-            jax.ShapeDtypeStruct((1,), f32),
+            jax.ShapeDtypeStruct((1,), jnp.int32),
+            jax.ShapeDtypeStruct((2, support, BS), f32),
         ),
-        in_specs=[smem, vmem, vmem, vmem, vmem],
-        out_specs=(vmem, smem),
+        in_specs=[hbm] * 5,
+        out_specs=(vmem, hbm, vmem),
         scratch_shapes=[
+            pltpu.SMEM((1,), f32),
+            pltpu.VMEM(block_coords.shape[::-1], jnp.int32),
+            pltpu.VMEM(band_vectors.shape, f32),
+            pltpu.VMEM(band_blocks.shape, jnp.int32),
+            dma((8,)),
+            pltpu.SMEM((1,), jnp.int32),
             pltpu.VMEM((2, support, BS), f32),
             pltpu.VMEM((16, 2, support, BS), f32),
-            pltpu.VMEM((64, *block), f32),
-            pltpu.VMEM((64, *block), f32),
-            pltpu.VMEM((64, *block), f32),
-            pltpu.VMEM((SLOTS, *block), f32),
-            pltpu.VMEM((SLOTS, *block), f32),
+            pltpu.VMEM((16 * ROWS, BS), f32),
+            pltpu.VMEM((16 * ROWS, BS), f32),
+            pltpu.VMEM((16 * ROWS, BS), f32),
+            pltpu.VMEM((ROWS, BS), f32),
+            pltpu.VMEM((ROWS, BS), f32),
             pltpu.VMEM((SLOTS, 16, BS), f32),
             pltpu.VMEM((SLOTS, 16, BS), f32),
             pltpu.VMEM((ROOM, 16, BS), f32),
@@ -610,16 +658,20 @@
             dma((1,)),
         ],
         compiler_params=pltpu.CompilerParams(
-            collective_id=0, has_side_effects=True, vmem_limit_bytes=28 << 20
+            collective_id=0, has_side_effects=True
         ),
         name="sparse",
-    )(spread.reshape(1), block_coords.T, core_blocks, band_vectors, band_blocks)
+    )(spread.reshape(1), block_coords.T, core_blocks.reshape(ROWS, BS), band_vectors, band_blocks)
 
 
 def on_device(core_blocks, block_coords, band_vectors, band_blocks, spread):
-    arguments = (core_blocks, block_coords, band_vectors, band_blocks, spread)
-    purified, most = sparse(*arguments)
-    return lax.cond(most[0] <= ROOM, lambda: purified, lambda: general(*arguments))
+    purified, fits, band = sparse(core_blocks, block_coords, band_vectors, band_blocks, spread)
+
+    def any_pattern():
+        blocks = band[1:, :, 0].astype(jnp.int32)
+        return general(core_blocks, block_coords, band[:1], blocks, spread)
+
+    return lax.switch(fits[0], [any_pattern, lambda: purified])
 
 
 def solution(mesh):

time: 66.6 us -> 65 us (0.976)
  Pallas kernels: 63.7 us -> 62.5 us
    pallas_call x1, Pallas kernels: 63.7 us -> 62.5 us  [sparse(): pl.pallas_call(kernel, out_shape=(jax.ShapeDtypeStruct(core_blocks.shape,...]
    unnamed x9 -> x5, local copies, waits for them, and re-layouts: 1.34 us -> 0.71 us
where the time goes in v4:
time: 65 us; the launch traced here: 64.9 us
  Pallas kernels  62.5 us (96%)
  between operations  1.43 us (2%)
  local copies, waits for them, and re-layouts  0.71 us (1%)
    pallas_call x1, Pallas kernels, sparse(): pl.pallas_call(kernel, out_shape=(jax.ShapeDtypeStruct(core_blocks.shape,...  62.5 us

profile of v4, /device:TPU:1, one launch (start us, length us, event | category | flops | bytes accessed | tf_op | source)
XLA Modules:
  0.0 64.9 jit_solution(647559364183251434)
XLA Ops:
  0.0 0.0 copy-start
  0.7 0.0 copy-start.1
  0.7 62.5 %sparse.1 = (f32[4,128,128]{2,1,0:T(8,128)S(1)}, s32[1]{0:T(128)}, f32[2,16,128]{2,1,0:T(8,128)S(1)}) custom-call(f32[1]{0:T(128)} %bitcast.148.spread_hbm, s32[32,64]{1,0:T(8,128)} %bitcast.154, f32[512,128]{1,0:T(8,128)} %bitcast.149, f32[1,16,128]{2,1,0:T(8,128)} %vector_hbm.1, s32[1,16]{1,0:T(1,128)} %block_hbm.1), custom_call_target="tpu_custom_call" | custom-call | tf_op jit(solution)/shard_map/sparse/pallas_call | solution.py:617
  63.9 0.0 copy-done
  63.9 0.0 copy-done.1
  63.9 0.2 conditional.1
  64.2 0.7 %copy.81 = f32[4,128,128]{2,1,0:T(8,128)} copy(f32[4,128,128]{2,1,0:T(8,128)S(1)} %get-tuple-element.546) | data formatting | bytes 524288
Async XLA Ops:
  0.0 63.9 %copy-start = (f32[4,128,128]{2,1,0:T(8,128)S(1)}, f32[4,128,128]{2,1,0:T(8,128)}, u32[]{:S(2)}) copy-start(f32[4,128,128]{2,1,0:T(8,128)} %param.11) | copy-start | bytes 786436
  0.7 63.2 %copy-start.1 = (s32[64,32]{0,1:T(8,128)S(1)}, s32[64,32]{0,1:T(8,128)}, u32[]{:S(2)}) copy-start(s32[64,32]{0,1:T(8,128)} %param.12) | copy-start | bytes 24580

commit v5 on v4

--- a/solution.py
+++ b/solution.py
@@ -18,7 +18,7 @@
 ROOM = 20
 PAD = 256
 ROWS = SLOTS * BS
-EARLY = 240
+EARLY = 256
 EARLY_SQUARE = 272
 
 highest = lax.Precision.HIGHEST

time: 65 us -> 64.9 us (level)
  no operation moved by 1% of the time
where the time goes in v5:
time: 64.9 us
  Pallas kernels  62.5 us (96%)
  between operations  1.43 us (2%)
  local copies, waits for them, and re-layouts  0.71 us (1%)
    pallas_call x1, Pallas kernels, sparse(): pl.pallas_call(kernel, out_shape=(jax.ShapeDtypeStruct(core_blocks.shape,...  62.5 us

profile of v5, /device:TPU:1, one launch (start us, length us, event | category | flops | bytes accessed | tf_op | source)
XLA Modules:
  0.0 64.9 jit_solution(15786467329855315530)
XLA Ops:
  0.0 0.0 copy-start
  0.7 0.0 copy-start.1
  0.7 62.5 %sparse.1 = (f32[4,128,128]{2,1,0:T(8,128)S(1)}, s32[1]{0:T(128)}, f32[2,16,128]{2,1,0:T(8,128)S(1)}) custom-call(f32[1]{0:T(128)} %bitcast.148.spread_hbm, s32[32,64]{1,0:T(8,128)} %bitcast.154, f32[512,128]{1,0:T(8,128)} %bitcast.149, f32[1,16,128]{2,1,0:T(8,128)} %vector_hbm.1, s32[1,16]{1,0:T(1,128)} %block_hbm.1), custom_call_target="tpu_custom_call" | custom-call | tf_op jit(solution)/shard_map/sparse/pallas_call | solution.py:617
  63.9 0.0 copy-done
  63.9 0.0 copy-done.1
  63.9 0.2 conditional.1
  64.1 0.7 %copy.81 = f32[4,128,128]{2,1,0:T(8,128)} copy(f32[4,128,128]{2,1,0:T(8,128)S(1)} %get-tuple-element.546) | data formatting | bytes 524288
Async XLA Ops:
  0.0 63.9 %copy-start = (f32[4,128,128]{2,1,0:T(8,128)S(1)}, f32[4,128,128]{2,1,0:T(8,128)}, u32[]{:S(2)}) copy-start(f32[4,128,128]{2,1,0:T(8,128)} %param.11) | copy-start | bytes 786436
  0.7 63.2 %copy-start.1 = (s32[64,32]{0,1:T(8,128)S(1)}, s32[64,32]{0,1:T(8,128)}, u32[]{:S(2)}) copy-start(s32[64,32]{0,1:T(8,128)} %param.12) | copy-start | bytes 24580
